TPU v7x, 512 devices: a whole 4x4x16 slice. The times are simulated.
512 devices in a mesh: field: 32 (over z_hi, x, core), point: 16 (over y, z_lo).
Axes of the slice: x: 4, y: 4, z: 16 (z_hi: 4, z_lo: 4; z = z_hi * 4 + z_lo), core: 2. Of those that a mesh axis runs over, the one named last changes fastest.
Arguments:
- residual_in: bfloat16 [32, 4096, 2048], P('field', 'point'), may hold values from -6 to 6
- coefs_in: bfloat16 [32, 4096, 4, 256], P('field', 'point'), may hold values from 0 to 1
- dictionary: bfloat16 [8192, 2048], P('field'), may hold values from -0.125 to 0.125
- owner_order: int32 [32], replicated, may hold values from 0 to 31, each once
- pixel_of: int32 [32, 4096], P('field', 'point'), may hold values from 0 to 4095, each once within a row
Outputs:
- maps: float32 [32, 4, 256, 32, 128], P('field', None, 'point')
Inputs may be any that keep to these rules, and one draw needn't show every extreme that they name: `owner_order`: A permutation of the dictionary blocks. `pixel_of`: each field's row is a permutation of its scan points over the 32 x 128 pixels.
All inputs are finite; a program needn't handle non-finite values.
Results may differ from a plain program's by a relative error of at most 0.00045.
Values may be sent and summed in bfloat16 or wider, within the bound.
A program may use at most 64 MiB of HBM per device.

v0:
```python
import jax
import jax.numpy as jnp
from jax import lax
from jax.sharding import PartitionSpec as P

TURNS = 4
SWEEPS = 4
MAP_W = 128


time_step = 0.2
edge_scale = 0.5


def from_root(value, axis, source):
    kept = jnp.where(lax.axis_index(axis) == source, value, 0).astype(value.dtype)
    return lax.psum(kept, axis)


def block_steps(templates):
    gram = lax.dot_general(
        templates, templates, (((1,), (1,)), ((), ())), preferred_element_type=jnp.float32
    )
    return 1.0 / jnp.sum(jnp.abs(gram), axis=1)


def diffuse(grids):
    for repeat in range(SWEEPS):
        padded = jnp.pad(grids, ((0, 0), (1, 1), (1, 1)), mode="edge")
        summed = jnp.zeros_like(grids)
        for neighbour in (
            padded[:, :-2, 1:-1],
            padded[:, 2:, 1:-1],
            padded[:, 1:-1, :-2],
            padded[:, 1:-1, 2:],
        ):
            differ = neighbour - grids
            scaled = differ / edge_scale
            summed = summed + differ / (1.0 + scaled * scaled)
        grids = grids + time_step * summed
    return grids


def build_maps(moved, pixel_ids):
    points = moved.shape[0]
    count = moved.shape[1]
    local_kb = moved.shape[2]
    values = moved.reshape(points, count * local_kb).T
    flat = jnp.zeros((count * local_kb, points), jnp.float32).at[:, pixel_ids].set(values)
    grids = diffuse(flat.reshape(count * local_kb, points // MAP_W, MAP_W))
    return grids.reshape(count, local_kb, points // MAP_W, MAP_W)


def per_device(residual_in, coefs_in, dictionary, owner_order, pixel_of):
    residual = residual_in[0]
    coefs = coefs_in[0].astype(jnp.float32)
    pixel_ids = lax.all_gather(pixel_of[0], "point", axis=0, tiled=True)
    updated = []
    for turn_index in range(TURNS):
        owner = owner_order[turn_index]
        templates = from_root(dictionary, "field", owner)
        step_size = block_steps(templates)
        correlation = lax.dot_general(
            residual, templates, (((1,), (1,)), ((), ())), preferred_element_type=jnp.float32
        )
        before = coefs[:, turn_index, :]
        after = jnp.maximum(before + step_size[None, :] * correlation, 0.0)
        updated.append(after)
        if turn_index + 1 < TURNS:
            change = (after - before).astype(jnp.bfloat16)
            residual = (
                residual.astype(jnp.float32)
                - jnp.dot(change, templates, preferred_element_type=jnp.float32)
            ).astype(jnp.bfloat16)
    stacked = jnp.stack(updated, axis=1)
    maps = build_maps(
        lax.all_to_all(stacked, "point", split_axis=2, concat_axis=0, tiled=True), pixel_ids
    )
    return maps[None]


def solution(mesh):
    placed = (
        P("field", "point", None),
        P("field", "point", None, None),
        P("field", None),
        P(),
        P("field", "point"),
    )
    return jax.shard_map(
        per_device,
        mesh=mesh,
        in_specs=placed,
        out_specs=P("field", None, "point", None, None),
        check_vma=False,
    )
```

profile of v0, /device:TPU:1, one launch (start us, length us, event | category | flops | bytes accessed | tf_op | source)
XLA Modules:
  0.0 498.6 jit_solution(4180003535699886071)
XLA Ops:
  6.5 0.0 all-reduce.3.cloned.1.call-start
  6.5 1.5 fusion.46
  10.5 3.3 broadcast_select_fusion.3
  13.8 0.0 copy-start.4
  13.9 0.0 all-reduce.3.cloned.1.call-update
  13.9 1.0 copy-done.4
  14.9 0.3 copy.27
  15.2 0.1 bitcast_convert_fusion
  15.3 0.0 copy-start
  15.3 380.9 %all-reduce.3.cloned.1.call-done = (bf16[256,2048]{1,0:T(8,128)(2,1)}, bf16[256,2048]{1,0:T(8,128)(2,1)}, bf16[256,2048]{1,0:T(8,128)(2,1)}, bf16[256,2048]{1,0:T(8,128)(2,1)}) async-done(((bf16[256,2048]{1,0:T(8,128)(2,1)}, bf16[256,2048]{1,0:T(8,128)(2,1)}, bf16[256,2048]{1,0:T(8,128)(2,1)}, bf16[256,2048]{1,0:T(8,128)(2,1)}), (bf16[256,2048]{1,0:T(8,128)(2,1)}, bf16[256,2048]{1,0:T(8,128)(2,1)}, ...) | async-done | bytes 4194320 | tf_op jit(solution)/shard_map/psum | solution.py:17
  396.3 0.0 copy-start.2
  396.3 2.1 fusion.15
  398.4 0.0 copy-done
  398.4 0.0 copy-done.2
  398.4 0.5 fusion.14
  398.9 0.0 copy-start.1
  398.9 0.5 fusion
  399.4 0.7 copy-done.1
  400.1 0.5 fusion.16
  400.6 0.5 fusion.11
  401.1 0.0 copy-start.3
  401.1 0.5 fusion.1
  401.6 0.0 copy-start.6
  401.6 0.7 copy-done.3
  402.3 0.5 fusion.17
  402.8 0.1 copy-done.6
  402.9 0.5 fusion.18
  403.4 0.5 fusion.9
  403.9 2.5 fusion.7
  406.4 0.1 pad_maximum_fusion.36
  406.4 1.6 copy.31
  408.1 0.0 copy-start.5
  408.1 8.7 %all-to-all-start = ((f32[256,4,256]{0,1,2:T(4,128)}), f32[256,4,256]{0,1,2:T(4,128)S(1)}, u32[]{:S(2)}, u32[]{:S(2)}) async-start(f32[256,4,256]{0,1,2:T(4,128)} %copy.31), calls=%async_computation | async-start | bytes 2097152 | tf_op jit(solution)/shard_map/all_to_all | solution.py:77
  416.8 0.0 copy-done.5
  416.8 47.6 %all-gather = s32[1,4096]{1,0:T(1,128)S(1)} all-gather(s32[1,256]{1,0:T(1,128)S(1)} %copy-done.5), channel_id=2, replica_groups=mesh['field'=32,'point'=16] {'point'}, dimensions={1}, use_global_device_ids=true | all-gather | bytes 17408 | tf_op jit(solution)/shard_map/all_gather | solution.py:57
  464.4 0.0 all-to-all-done
  464.4 0.6 copy.32
  465.1 0.6 copy.39
  465.7 2.0 copy.33
  467.6 11.6 %scatter_custom_fusion = f32[64,4096]{0,1:T(8,128)S(1)} fusion(s32[4096]{0:T(1024)S(1)} %compare_select_fusion, f32[4096,64]{1,0:T(8,128)} %copy.33, f32[]{:T(128)} %constant.31.clone.1), kind=kCustom, calls=%fused_computation.88 | custom fusion | bytes 1049088 | tf_op jit(solution)/shard_map/scatter | solution.py:49
  479.2 0.9 copy.38
  480.2 0.1 fusion.45
  480.3 0.2 pad_maximum_fusion
  480.5 0.4 fusion.41
  480.9 2.0 multiply_add_fusion.3
  483.0 0.2 pad_maximum_fusion.1
  483.2 0.4 fusion.40
  483.6 2.0 multiply_add_fusion.2
  485.6 0.2 pad_maximum_fusion.2
  485.9 0.4 fusion.39
  486.3 2.0 multiply_add_fusion.1
  488.3 0.2 pad_maximum_fusion.3
  488.5 0.4 fusion.38
  489.0 2.8 multiply_add_fusion
  (8 shorter events, 0.2 us)
Async XLA Ops:
  6.5 389.7 %all-reduce.3.cloned.1.call-start = ((), (), s32[]{:S(2)}) async-start(), calls=%async_computation.1 | async-start | bytes 8388608 | tf_op jit(solution)/shard_map/psum | solution.py:17
  13.8 1.0 copy-start.4
  15.3 383.1 %copy-start = (bf16[1,256,2048]{2,1,0:T(8,128)(2,1)S(1)}, bf16[1,256,2048]{2,1,0:T(8,128)(2,1)}, u32[]{:S(2)}) copy-start(bf16[1,256,2048]{2,1,0:T(8,128)(2,1)} %param.5) | copy-start | bytes 3145732
  396.3 2.1 copy-start.2
  398.9 1.2 copy-start.1
  401.1 1.2 copy-start.3
  401.6 1.3 copy-start.6
  408.1 8.7 %copy-start.5 = (s32[1,256]{1,0:T(1,128)S(1)}, s32[1,256]{1,0:T(1,128)}, u32[]{:S(2)}) copy-start(s32[1,256]{1,0:T(1,128)} %param.9) | copy-start | bytes 3076
  408.1 56.3 %all-to-all-start = ((f32[256,4,256]{0,1,2:T(4,128)}), f32[256,4,256]{0,1,2:T(4,128)S(1)}, u32[]{:S(2)}, u32[]{:S(2)}) async-start(f32[256,4,256]{0,1,2:T(4,128)} %copy.31), calls=%async_computation | async-start | bytes 2097152 | tf_op jit(solution)/shard_map/all_to_all | solution.py:77
Sparse Core Ops, SparseCore 0:
  14.0 382.2 all-reduce.2
where the time goes:
time: 503 us; the launch traced here: 499 us
  waiting for transfers between devices  381 us (76%)
  blocking collectives  47.6 us (9%)
  local copies, waits for them, and re-layouts  23.6 us (5%)
  between operations  16.2 us (3%)
  other arithmetic  13.1 us (3%)
  starting transfers between devices  8.71 us (2%)
  matrix products  8.38 us (2%)
    psum x1, waiting for transfers between devices, from_root(): return lax.psum(kept, axis)  381 us
    all_gather x1, blocking collectives, per_device(): pixel_ids = lax.all_gather(pixel_of[0], 'point', axis=0, tiled=True)  47.6 us
    scatter x1, local copies, waits for them, and re-layouts, build_maps(): jnp.zeros((count * local_kb, points), jnp.float32).at[:, pixel_ids]  11.6 us
  transfers between devices with their start and end apart: 2, of which 1 were waited for; matrix products, arithmetic and copies ran while one was open for 0% of the time, Pallas kernels for 0%

commit v1 on v0

--- a/solution.py
+++ b/solution.py
@@ -1,20 +1,217 @@
+import functools
+
 import jax
 import jax.numpy as jnp
 from jax import lax
+from jax.experimental import pallas as pl
+from jax.experimental.pallas import tpu as pltpu
 from jax.sharding import PartitionSpec as P
 
 TURNS = 4
 SWEEPS = 4
 MAP_W = 128
-
+MESH = pl.DeviceIdType.MESH
 
 time_step = 0.2
 edge_scale = 0.5
 
 
-def from_root(value, axis, source):
-    kept = jnp.where(lax.axis_index(axis) == source, value, 0).astype(value.dtype)
-    return lax.psum(kept, axis)
+def dev(z, x, core, y):
+    return (z // 4 * 8 + x * 2 + core, y * 4 + z % 4)
+
+
+def remote(src, dst, send, recv, device):
+    return pltpu.make_async_remote_copy(
+        src_ref=src, dst_ref=dst, send_sem=send, recv_sem=recv, device_id=device, device_id_type=MESH
+    )
+
+
+def gather_kernel(
+    owner, block, g, cand, a_send, a_recv, b_send, b_recv, own_sem, z_send, z_recv, ring_send, ring_recv, c_send, c_recv
+):
+    f = lax.axis_index("field")
+    p = lax.axis_index("point")
+    core = f % 2
+    chip = f // 2
+    x = chip % 4
+    zh = f // 8
+    y = p // 4
+    z = zh * 4 + p % 4
+    sibling = (f + 1 - 2 * core, p)
+
+    barrier = pltpu.get_barrier_semaphore()
+
+    def greet(device):
+        pl.semaphore_signal(barrier, inc=1, device_id=device, device_id_type=MESH)
+
+    def greet_field(i, _):
+        greet(((chip + i) % 16 * 2 + core, p))
+        return _
+
+    lax.fori_loop(1, 16, greet_field, 0)
+
+    def greet_z(i, _):
+        @pl.when(i % 4 != 0)
+        def _greet():
+            greet(dev((z + i) % 16, x, core, y))
+
+        return _
+
+    lax.fori_loop(1, 16, greet_z, 0)
+    for step in (1, 3):
+        greet(dev(z, x, core, (y + step) % 4))
+    greet(sibling)
+    pl.semaphore_wait(barrier, 15 + 12 + 2 + 1)
+
+    lanes = pl.ds(pl.multiple_of(p * 128, 128), 128)
+
+    def tile_of(to):
+        return block.at[pl.ds(pl.multiple_of(to * 16, 16), 16), lanes]
+
+    def scatter(i, _):
+        to = (chip + i) % 16
+        remote(tile_of(to), cand.at[core, chip], a_send, a_recv, (to * 2 + core, p)).start()
+        return _
+
+    lax.fori_loop(1, 16, scatter, 0)
+    own = pltpu.make_async_copy(tile_of(chip), cand.at[core, chip], own_sem)
+    own.start()
+    own.wait()
+    all_a = remote(cand.at[0, pl.ds(0, 15)], cand.at[0, pl.ds(0, 15)], a_send, a_recv, sibling)
+    all_a.wait_recv()
+    both = remote(cand.at[core], cand.at[core], b_send, b_recv, sibling)
+    both.start()
+    all_a.wait_send()
+    both.wait()
+
+    mine = pl.ds(pl.multiple_of(x * 16, 16), 16)
+    for tt in range(2):
+        o = owner[core + 2 * tt]
+        g[core, tt, p, zh, mine, :] = cand[o % 2, o // 2]
+
+    def along_z(i, _):
+        part = g.at[core, :, p, zh, mine, :]
+        remote(part, part, z_send, z_recv, dev((z + i) % 16, x, core, y)).start()
+        return _
+
+    lax.fori_loop(1, 16, along_z, 0)
+    amount = g.at[0, 0, pl.ds(0, 15), 0, pl.ds(0, 32), :]
+    all_z = remote(amount, amount, z_send, z_recv, sibling)
+    all_z.wait_recv()
+    all_z.wait_send()
+
+    def ring(stage, neighbour, region):
+        def make(t, kind):
+            offset, half, to = ((0, None, 1), (0, None, 3), (3, 0, 1), (1, 1, 3))[kind]
+            ref = g.at[region(t, offset, half)]
+            return remote(ref, ref, ring_send.at[stage, kind, t], ring_recv.at[stage, kind, t], neighbour(to))
+
+        def start(t):
+            make(t, 0).start()
+            make(t, 1).start()
+
+        def forward(t):
+            make(t, 0).wait_recv()
+            make(t, 2).start()
+            make(t, 1).wait_recv()
+            make(t, 3).start()
+
+        def finish(t):
+            make(t, 2).wait_recv()
+            make(t, 3).wait_recv()
+
+        def drain(t):
+            for kind in range(4):
+                make(t, kind).wait_send()
+
+        return start, forward, finish, drain
+
+    def along(axis):
+        def neighbour(step):
+            if axis == "x":
+                return dev(z, (x + step) % 4, core, y)
+            return dev(z, x, core, (y + step) % 4)
+
+        return neighbour
+
+    def mid_region(axis):
+        def region(t, offset, half):
+            bx = (x + offset) % 4 if axis == "x" else x
+            by = (y + offset) % 4 if axis == "y" else y
+            points = pl.ds(by * 4, 4) if half is None else pl.ds(by * 4 + 2 * half, 2)
+            return (core, t // 2, points, pl.ds(t % 2 * 2, 2), pl.ds(pl.multiple_of(bx * 16, 16), 16), slice(None))
+
+        return region
+
+    def last_region(axis):
+        def region(t, offset, half):
+            if axis == "x":
+                points = pl.ds(0, 16) if half is None else pl.ds(8 * half, 8)
+                rows = pl.ds(pl.multiple_of((x + offset) % 4 * 16, 16), 16)
+            else:
+                by = (y + offset) % 4
+                points = pl.ds(by * 4, 4) if half is None else pl.ds(by * 4 + 2 * half, 2)
+                rows = slice(None)
+            return (core, t // 2, points, pl.ds(t % 2 * 2, 2), rows, slice(None))
+
+        return region
+
+    def swap(t):
+        part = g.at[core, t // 2, :, pl.ds(t % 2 * 2, 2)]
+        return remote(part, part, c_send.at[t], c_recv.at[t], sibling)
+
+    def rings(first, last):
+        m_start, m_forward, m_finish, m_drain = ring(0, along(first), mid_region(first))
+        l_start, l_forward, l_finish, l_drain = ring(1, along(last), last_region(last))
+        for t in range(TURNS):
+            m_start(t)
+        for t in range(TURNS):
+            m_forward(t)
+            m_finish(t)
+            l_start(t)
+        for t in range(TURNS):
+            l_forward(t)
+            l_finish(t)
+            swap(t).start()
+        for t in range(TURNS):
+            m_drain(t)
+            l_drain(t)
+
+    @pl.when(core == 0)
+    def _even():
+        rings("y", "x")
+
+    @pl.when(core == 1)
+    def _odd():
+        rings("x", "y")
+
+    for t in range(TURNS):
+        swap(t).wait()
+
+
+def gather_blocks(owner_order, dictionary):
+    return pl.pallas_call(
+        gather_kernel,
+        name="gather_blocks",
+        out_shape=jax.ShapeDtypeStruct((2, 2, 16, 4, 64, 128), jnp.bfloat16),
+        in_specs=[pl.BlockSpec(memory_space=pltpu.SMEM), pl.BlockSpec(memory_space=pl.ANY)],
+        out_specs=pl.BlockSpec(memory_space=pltpu.VMEM),
+        scratch_shapes=[
+            pltpu.VMEM((2, 16, 16, 128), jnp.bfloat16),
+            pltpu.SemaphoreType.DMA,
+            pltpu.SemaphoreType.DMA,
+            pltpu.SemaphoreType.DMA,
+            pltpu.SemaphoreType.DMA,
+            pltpu.SemaphoreType.DMA,
+            pltpu.SemaphoreType.DMA,
+            pltpu.SemaphoreType.DMA,
+            pltpu.SemaphoreType.DMA((2, 4, TURNS)),
+            pltpu.SemaphoreType.DMA((2, 4, TURNS)),
+            pltpu.SemaphoreType.DMA((TURNS,)),
+            pltpu.SemaphoreType.DMA((TURNS,)),
+        ],
+        compiler_params=pltpu.CompilerParams(collective_id=0, has_side_effects=True, vmem_limit_bytes=16 << 20),
+    )(owner_order, dictionary)
 
 
 def block_steps(templates):
@@ -56,9 +253,9 @@
     coefs = coefs_in[0].astype(jnp.float32)
     pixel_ids = lax.all_gather(pixel_of[0], "point", axis=0, tiled=True)
     updated = []
+    gathered = gather_blocks(owner_order, dictionary)
     for turn_index in range(TURNS):
-        owner = owner_order[turn_index]
-        templates = from_root(dictionary, "field", owner)
+        templates = gathered[turn_index % 2, turn_index // 2].transpose(1, 2, 0, 3).reshape(256, 2048)
         step_size = block_steps(templates)
         correlation = lax.dot_general(
             residual, templates, (((1,), (1,)), ((), ())), preferred_element_type=jnp.float32

time: 503 us -> 183 us (0.36)
  the two profiles are of different devices: /device:TPU:1 before, /device:TPU:2 now
where the time goes in v1:
time: 183 us
  Pallas kernels  75 us (41%)
  blocking collectives  55.5 us (30%)
  local copies, waits for them, and re-layouts  29.2 us (16%)
  other arithmetic  10.9 us (6%)
  matrix products  6.78 us (4%)
  starting transfers between devices  4.92 us (3%)
    pallas_call x1, Pallas kernels, gather_blocks(): pl.pallas_call(gather_kernel, name='gather_blocks', out_shape=jax.ShapeDt...  75 us
    all_gather x1, blocking collectives, per_device(): pixel_ids = lax.all_gather(pixel_of[0], 'point', axis=0, tiled=True)  55.5 us
    scatter x1, local copies, waits for them, and re-layouts, build_maps(): jnp.zeros((count * local_kb, points), jnp.float32).at[:, pixel_ids]  11.4 us
    add x4, other arithmetic, diffuse(): grids = grids + time_step * summed  8.81 us
    unnamed x20, local copies, waits for them, and re-layouts  5.69 us
    transpose x5, local copies, waits for them, and re-layouts, per_device(): gathered[turn_index % 2, turn_index // 2].transpose(1, 2, 0, 3)  5.11 us
    all_to_all x1, starting transfers between devices, per_device(): lax.all_to_all(stacked, 'point', split_axis=2, concat_axis=0, tiled=True)  4.92 us
    dot_general x4, matrix products, per_device(): lax.dot_general(residual, templates, (((1,), (1,)), ((), ())), preferred_...  3.79 us
  transfers between devices with their start and end apart: 1, of which 0 were waited for; matrix products, arithmetic and copies ran while one was open for 0% of the time, Pallas kernels for 0%

profile of v1, /device:TPU:2, one launch (start us, length us, event | category | flops | bytes accessed | tf_op | source)
XLA Modules:
  0.0 182.7 jit_solution(15225347428128231418)
XLA Ops:
  0.0 0.0 copy-start
  0.0 1.2 copy-done
  1.2 0.0 copy-start.1
  1.2 0.7 copy-done.1
  1.9 75.0 %gather_blocks.1 = bf16[2,2,16,4,64,128]{5,4,3,2,1,0:T(8,128)(2,1)S(1)} custom-call(s32[32]{0:T(128)S(1)} %copy-done.1, bf16[256,2048]{1,0:T(8,128)(2,1)S(1)} %copy-done), custom_call_target="tpu_custom_call" | custom-call | tf_op jit(solution)/shard_map/gather_blocks/pallas_call | solution.py:193
  76.9 2.4 %slice_bitcast_fusion.1 = (bf16[4,64,16,128]{3,1,0,2:T(8,128)(2,1)S(1)}, bf16[4,64,16,128]{3,1,0,2:T(8,128)(2,1)S(1)}, bf16[4,64,16,128]{3,1,0,2:T(8,128)(2,1)}, bf16[4,64,16,128]{3,1,0,2:T(8,128)(2,1)S(1)}) fusion(bf16[2,2,16,4,64,128]{5,4,3,2,1,0:T(8,128)(2,1)S(1)} %gather_blocks.1), kind=kLoop, calls=%fused_computation.100 | loop fusion | bytes 8388608 | tf_op jit(solution)/shard_map/transpose | solution.py:258
  79.3 0.7 copy.36
  80.0 0.5 fusion.15
  80.5 2.1 %copy.35 = bf16[1,256,4,256]{1,3,2,0:T(8,128)(2,1)} copy(bf16[1,256,4,256]{3,2,1,0:T(4,128)(2,1)} %param.6) | data formatting | bytes 1048576 | tf_op args[1]
  82.6 0.0 copy-start.4
  82.6 1.2 bitcast_convert_fusion
  83.8 0.2 copy-done.4
  84.0 0.0 copy-start.3
  84.0 0.5 fusion.14
  84.5 0.0 copy-start.2
  84.5 0.5 fusion
  85.0 0.7 copy-done.2
  85.7 0.7 copy.37
  86.4 0.5 fusion.16
  86.9 0.5 fusion.11
  87.4 0.0 copy-start.5
  87.4 0.5 fusion.1
  87.9 0.2 copy-done.5
  88.1 0.7 copy.39
  88.8 0.0 copy-start.7
  88.8 0.5 fusion.17
  89.3 0.7 copy.41
  90.0 0.5 fusion.18
  90.5 0.0 copy-done.3
  90.5 0.0 copy-done.7
  90.6 0.5 fusion.9
  91.0 0.0 copy-start.6
  91.1 2.3 %fusion.7 = f32[256,1,256]{0,2,1:T(8,128)S(1)} fusion(bf16[256,2048]{1,0:T(8,128)(2,1)S(1)} %fusion.1, bf16[32,8,16,128]{3,2,1,0:T(8,128)(2,1)S(1)} %bitcast.123, bf16[32,8,16,128]{3,2,1,0:T(8,128)(2,1)} %bitcast.121, f32[256,4,256]{0,2,1:T(8,128)} %copy-done.3, f32[256,256]{0,1:T(8,128)S(1)} %fusion.9, f32[256]{0:T(256)S(1)} %broadcast_divide_fusion), kind=kOutput, calls=%fused_computation.15 | convolution fusion | flops 538771456 | bytes 4195328 | tf_op jit(solution)/shard_map/dot_general | solution.py:260
  93.4 0.0 copy-done.6
  93.4 0.1 pad_maximum_fusion.36
  93.5 1.6 copy.43
  95.2 0.0 copy-start.8
  95.2 4.9 %all-to-all-start = ((f32[256,4,256]{0,1,2:T(4,128)}), f32[256,4,256]{0,1,2:T(4,128)S(1)}, u32[]{:S(2)}, u32[]{:S(2)}) async-start(f32[256,4,256]{0,1,2:T(4,128)} %copy.43), calls=%async_computation | async-start | bytes 2097152 | tf_op jit(solution)/shard_map/all_to_all | solution.py:274
  100.1 0.0 copy-done.8
  100.1 55.5 %all-gather = s32[1,4096]{1,0:T(1,128)S(1)} all-gather(s32[1,256]{1,0:T(1,128)S(1)} %copy-done.8), channel_id=2, replica_groups=mesh['field'=32,'point'=16] {'point'}, dimensions={1}, use_global_device_ids=true | all-gather | bytes 17408 | tf_op jit(solution)/shard_map/all_gather | solution.py:254
  155.6 0.0 all-to-all-done
  155.6 0.6 copy.44
  156.2 0.6 copy.55
  156.8 2.0 %copy.45 = f32[4096,64]{1,0:T(8,128)} copy(f32[4096,64]{0,1:T(8,128)S(1)} %bitcast.114) | data formatting | bytes 2097152 | tf_op jit(solution)/shard_map/reshape | solution.py:245
  158.8 11.4 %scatter_custom_fusion = f32[64,4096]{0,1:T(8,128)S(1)} fusion(s32[4096]{0:T(1024)S(1)} %compare_select_fusion, f32[4096,64]{1,0:T(8,128)} %copy.45, f32[]{:T(128)} %constant.25.clone.1), kind=kCustom, calls=%fused_computation.103 | custom fusion | bytes 1049088 | tf_op jit(solution)/shard_map/scatter | solution.py:246
  170.2 0.9 copy.50
  171.2 0.1 fusion.69
  171.2 0.2 pad_maximum_fusion
  171.5 0.4 fusion.65
  171.9 2.0 %multiply_add_fusion.3 = f32[64,32,128]{2,1,0:T(8,128)S(1)} fusion(f32[64,32,128]{2,1,0:T(8,128)S(1)} %copy.50, f32[64,34,1]{2,1,0:T(8,128)S(1)} %get-tuple-element.16, f32[64,1,128]{2,1,0:T(1,128)S(1)} %get-tuple-element.24, f32[64,1,128]{2,1,0:T(1,128)S(1)} %get-tuple-element.23, f32[64,34,1]{2,1,0:T(8,128)S(1)} %get-tuple-element.15), kind=kLoop, calls=%fused_computation.98 | loop fusion | flops 8650752 | bytes 2180096 | tf_op jit(solution)/shard_map/add | solution.py:237
  174.0 0.2 pad_maximum_fusion.1
  174.2 0.4 fusion.64
  174.6 2.0 %multiply_add_fusion.2 = f32[64,32,128]{2,1,0:T(8,128)S(1)} fusion(f32[64,32,128]{2,1,0:T(8,128)S(1)} %multiply_add_fusion.3, f32[64,34,1]{2,1,0:T(8,128)S(1)} %get-tuple-element.14, f32[64,1,128]{2,1,0:T(1,128)S(1)} %get-tuple-element.22, f32[64,1,128]{2,1,0:T(1,128)S(1)} %get-tuple-element.21, f32[64,34,1]{2,1,0:T(8,128)S(1)} %get-tuple-element.13), kind=kLoop, calls=%fused_computation.97 | loop fusion | flops 8650752 | bytes 2180096 | tf_op jit(solution)/shard_map/add | solution.py:237
  176.6 0.2 pad_maximum_fusion.2
  176.8 0.4 fusion.63
  177.3 2.0 %multiply_add_fusion.1 = f32[64,32,128]{2,1,0:T(8,128)S(1)} fusion(f32[64,32,128]{2,1,0:T(8,128)S(1)} %multiply_add_fusion.2, f32[64,34,1]{2,1,0:T(8,128)S(1)} %get-tuple-element.12, f32[64,1,128]{2,1,0:T(1,128)S(1)} %get-tuple-element.20, f32[64,1,128]{2,1,0:T(1,128)S(1)} %get-tuple-element.19, f32[64,34,1]{2,1,0:T(8,128)S(1)} %get-tuple-element.11), kind=kLoop, calls=%fused_computation.96 | loop fusion | flops 8650752 | bytes 2180096 | tf_op jit(solution)/shard_map/add | solution.py:237
  179.3 0.2 pad_maximum_fusion.3
  179.5 0.4 fusion.62
  180.0 2.8 %multiply_add_fusion = f32[64,32,128]{2,1,0:T(8,128)} fusion(f32[64,32,128]{2,1,0:T(8,128)S(1)} %multiply_add_fusion.1, f32[64,34,1]{2,1,0:T(8,128)S(1)} %get-tuple-element.10, f32[64,1,128]{2,1,0:T(1,128)S(1)} %get-tuple-element.18, f32[64,1,128]{2,1,0:T(1,128)S(1)} %get-tuple-element.17, f32[64,34,1]{2,1,0:T(8,128)S(1)} %get-tuple-element.9), kind=kLoop, calls=%fused_computation.95 | loop fusion | flops 8650752 | bytes 2180096 | tf_op jit(solution)/shard_map/add | solution.py:237
  (8 shorter events, 0.2 us)
Async XLA Ops:
  0.0 1.2 copy-start
  1.2 0.7 copy-start.1
  82.6 1.4 copy-start.4
  84.0 6.5 %copy-start.3 = (f32[256,4,256]{0,2,1:T(8,128)}, f32[256,4,256]{0,2,1:T(8,128)S(1)}, u32[]{:S(2)}) copy-start(f32[256,4,256]{0,2,1:T(8,128)S(1)} %bitcast_convert_fusion) | copy-start | bytes 3145732
  84.5 1.2 copy-start.2
  87.4 0.7 copy-start.5
  88.8 1.7 copy-start.7
  91.0 2.4 %copy-start.6 = (f32[256,256]{0,1:T(8,128)S(1)}, f32[256,256]{0,1:T(8,128)}, u32[]{:S(2)}) copy-start(f32[256,256]{0,1:T(8,128)} %copy-done.5) | copy-start | bytes 786436
  95.2 4.9 %copy-start.8 = (s32[1,256]{1,0:T(1,128)S(1)}, s32[1,256]{1,0:T(1,128)}, u32[]{:S(2)}) copy-start(s32[1,256]{1,0:T(1,128)} %param.9) | copy-start | bytes 3076
  95.2 60.5 %all-to-all-start = ((f32[256,4,256]{0,1,2:T(4,128)}), f32[256,4,256]{0,1,2:T(4,128)S(1)}, u32[]{:S(2)}, u32[]{:S(2)}) async-start(f32[256,4,256]{0,1,2:T(4,128)} %copy.43), calls=%async_computation | async-start | bytes 2097152 | tf_op jit(solution)/shard_map/all_to_all | solution.py:274

commit v2 on v1

v2 whole, which is shorter than its diff:
```python
import functools

import jax
import jax.numpy as jnp
from jax import lax
from jax.experimental import pallas as pl
from jax.experimental.pallas import tpu as pltpu
from jax.sharding import PartitionSpec as P

TURNS = 4
SWEEPS = 4
MAP_W = 128
MESH = pl.DeviceIdType.MESH

time_step = 0.2
edge_scale = 0.5


def dev(z, x, core, y):
    return (z // 4 * 8 + x * 2 + core, y * 4 + z % 4)


def remote(src, dst, send, recv, device):
    return pltpu.make_async_remote_copy(
        src_ref=src, dst_ref=dst, send_sem=send, recv_sem=recv, device_id=device, device_id_type=MESH
    )


def nt(a, b):
    return lax.dot_general(a, b, (((1,), (1,)), ((), ())), preferred_element_type=jnp.float32)


def unmix_kernel(
    owner,
    block,
    residual_hbm,
    coefs,
    pixel_of,
    values,
    pixels,
    g,
    cand,
    residual,
    templates,
    updated,
    a_send,
    a_recv,
    b_send,
    b_recv,
    own_sem,
    z_send,
    z_recv,
    ring_send,
    ring_recv,
    c_send,
    c_recv,
    id_send,
    id_recv,
    v_send,
    v_recv,
    r_sem,
):
    f = lax.axis_index("field")
    p = lax.axis_index("point")
    core = f % 2
    chip = f // 2
    x = chip % 4
    zh = f // 8
    y = p // 4
    z = zh * 4 + p % 4
    sibling = (f + 1 - 2 * core, p)

    fetch = pltpu.make_async_copy(residual_hbm, residual, r_sem)
    fetch.start()
    barrier = pltpu.get_barrier_semaphore()

    def greet(device):
        pl.semaphore_signal(barrier, inc=1, device_id=device, device_id_type=MESH)

    def greet_field(i, _):
        greet(((chip + i) % 16 * 2 + core, p))
        return _

    lax.fori_loop(1, 16, greet_field, 0)

    def greet_z(i, _):
        @pl.when(i % 4 != 0)
        def _greet():
            greet(dev((z + i) % 16, x, core, y))

        return _

    lax.fori_loop(1, 16, greet_z, 0)

    def greet_point(i, _):
        to = (p + i) % 16

        @pl.when(to // 4 != y)
        def _greet():
            greet((f, to))

        return _

    lax.fori_loop(1, 16, greet_point, 0)
    greet(sibling)
    pl.semaphore_wait(barrier, 15 + 12 + 12 + 1)

    lanes = pl.ds(pl.multiple_of(p * 128, 128), 128)

    def tile_of(to):
        return block.at[pl.ds(pl.multiple_of(to * 16, 16), 16), lanes]

    def scatter(i, _):
        to = (chip + i) % 16
        remote(tile_of(to), cand.at[core, chip], a_send, a_recv, (to * 2 + core, p)).start()
        return _

    lax.fori_loop(1, 16, scatter, 0)

    def tell_pixels(i, _):
        remote(pixel_of, pixels.at[p], id_send, id_recv, (f, (p + i) % 16)).start()
        return _

    lax.fori_loop(1, 16, tell_pixels, 0)
    pixels[p] = pixel_of[...]
    own = pltpu.make_async_copy(tile_of(chip), cand.at[core, chip], own_sem)
    own.start()
    own.wait()
    all_a = remote(cand.at[0, pl.ds(0, 15)], cand.at[0, pl.ds(0, 15)], a_send, a_recv, sibling)
    all_a.wait_recv()
    both = remote(cand.at[core], cand.at[core], b_send, b_recv, sibling)
    both.start()
    all_a.wait_send()
    both.wait()

    mine = pl.ds(pl.multiple_of(x * 16, 16), 16)
    for tt in range(2):
        o = owner[core + 2 * tt]
        g[core, tt, p, zh, mine, :] = cand[o % 2, o // 2]

    def along_z(i, _):
        part = g.at[core, :, p, zh, mine, :]
        remote(part, part, z_send, z_recv, dev((z + i) % 16, x, core, y)).start()
        return _

    lax.fori_loop(1, 16, along_z, 0)
    amount = g.at[0, 0, pl.ds(0, 15), 0, pl.ds(0, 32), :]
    all_z = remote(amount, amount, z_send, z_recv, sibling)
    all_z.wait_recv()
    all_z.wait_send()

    def ring(stage, neighbour, region):
        def make(t, kind):
            offset, half, to = ((0, None, 1), (0, None, 3), (3, 0, 1), (1, 1, 3))[kind]
            ref = g.at[region(t, offset, half)]
            return remote(ref, ref, ring_send.at[stage, kind, t], ring_recv.at[stage, kind, t], neighbour(to))

        def start(t):
            make(t, 0).start()
            make(t, 1).start()

        def forward(t):
            make(t, 0).wait_recv()
            make(t, 2).start()
            make(t, 1).wait_recv()
            make(t, 3).start()

        def finish(t):
            make(t, 2).wait_recv()
            make(t, 3).wait_recv()

        def drain(t):
            for kind in range(4):
                make(t, kind).wait_send()

        return start, forward, finish, drain

    def along(axis):
        def neighbour(step):
            if axis == "x":
                return dev(z, (x + step) % 4, core, y)
            return dev(z, x, core, (y + step) % 4)

        return neighbour

    def mid_region(axis):
        def region(t, offset, half):
            bx = (x + offset) % 4 if axis == "x" else x
            by = (y + offset) % 4 if axis == "y" else y
            points = pl.ds(by * 4, 4) if half is None else pl.ds(by * 4 + 2 * half, 2)
            return (core, t // 2, points, pl.ds(t % 2 * 2, 2), pl.ds(pl.multiple_of(bx * 16, 16), 16), slice(None))

        return region

    def last_region(axis):
        def region(t, offset, half):
            if axis == "x":
                points = pl.ds(0, 16) if half is None else pl.ds(8 * half, 8)
                rows = pl.ds(pl.multiple_of((x + offset) % 4 * 16, 16), 16)
            else:
                by = (y + offset) % 4
                points = pl.ds(by * 4, 4) if half is None else pl.ds(by * 4 + 2 * half, 2)
                rows = slice(None)
            return (core, t // 2, points, pl.ds(t % 2 * 2, 2), rows, slice(None))

        return region

    def swap(t):
        part = g.at[core, t // 2, :, pl.ds(t % 2 * 2, 2)]
        return remote(part, part, c_send.at[t], c_recv.at[t], sibling)

    def rings(first, last):
        return ring(0, along(first), mid_region(first)), ring(1, along(last), last_region(last))

    def by_core(act):
        @pl.when(core == 0)
        def _even():
            act(*rings("y", "x"))

        @pl.when(core == 1)
        def _odd():
            act(*rings("x", "y"))

    def open_rings(mid, last):
        for t in range(TURNS):
            mid[0](t)
        for t in range(TURNS):
            mid[1](t)
            mid[2](t)
            last[0](t)

    def first_half(mid, last):
        for t in (0, 1):
            last[1](t)
            last[2](t)
            swap(t).start()

    def middle(mid, last):
        last[1](2)

    def second_half(mid, last):
        last[1](3)
        for t in (2, 3):
            last[2](t)
            swap(t).start()

    def close(mid, last):
        for t in range(TURNS):
            mid[3](t)
            last[3](t)

    def send_rows(t, to):
        rows = pl.ds(pl.multiple_of(to * 16, 16), 16)
        points = pl.ds(pl.multiple_of(p * 256, 256), 256)
        return updated.at[t, rows], values.at[t, :, points]

    def turn(t):
        for q in range(16):
            templates[:, 128 * q : 128 * (q + 1)] = g[t % 2, t // 2, q].reshape(256, 128)
        gram = nt(templates[...], templates[...])
        step = 1.0 / jnp.sum(jnp.abs(gram), axis=1, keepdims=True)
        before = coefs[t].astype(jnp.float32)
        after = jnp.maximum(before + step * nt(templates[...], residual[...]), 0.0)
        updated[t] = after

        def deliver(i, _):
            to = (p + i) % 16
            src, dst = send_rows(t, to)
            remote(src, dst, v_send.at[t], v_recv.at[t], (f, to)).start()
            return _

        lax.fori_loop(1, 16, deliver, 0)
        rows = pl.ds(pl.multiple_of(p * 16, 16), 16)
        values[t, :, pl.ds(pl.multiple_of(p * 256, 256), 256)] = updated[t, rows, :]
        if t + 1 < TURNS:
            change = (after - before).astype(jnp.bfloat16)
            for q in range(4):
                cols = slice(512 * q, 512 * (q + 1))
                moved = lax.dot_general(
                    change, templates[:, cols], (((0,), (0,)), ((), ())), preferred_element_type=jnp.float32
                )
                residual[:, cols] = (residual[:, cols].astype(jnp.float32) - moved).astype(jnp.bfloat16)

    by_core(open_rings)
    fetch.wait()
    by_core(first_half)
    swap(0).wait_recv()
    swap(1).wait_recv()
    turn(0)
    by_core(middle)
    turn(1)
    by_core(second_half)
    swap(2).wait_recv()
    swap(3).wait_recv()
    turn(2)
    turn(3)
    by_core(close)
    for t in range(TURNS):
        swap(t).wait_send()
    ids = remote(pixels.at[pl.ds(0, 15)], pixels.at[pl.ds(0, 15)], id_send, id_recv, sibling)
    ids.wait_send()
    ids.wait_recv()
    for t in range(TURNS):
        amount = values.at[t, :, pl.ds(0, 15 * 256)]
        done = remote(amount, amount, v_send.at[t], v_recv.at[t], sibling)
        done.wait_send()
        done.wait_recv()


def unmix(owner_order, dictionary, residual, coefs, pixel_of):
    vmem = pl.BlockSpec(memory_space=pltpu.VMEM)
    hbm = pl.BlockSpec(memory_space=pl.ANY)
    dma = pltpu.SemaphoreType.DMA
    return pl.pallas_call(
        unmix_kernel,
        name="unmix",
        out_shape=(
            jax.ShapeDtypeStruct((TURNS, 16, 4096), jnp.float32),
            jax.ShapeDtypeStruct((16, 1, 256), jnp.int32),
        ),
        in_specs=[pl.BlockSpec(memory_space=pltpu.SMEM), hbm, hbm, vmem, vmem],
        out_specs=(vmem, vmem),
        scratch_shapes=[
            pltpu.VMEM((2, 2, 16, 4, 64, 128), jnp.bfloat16),
            pltpu.VMEM((2, 16, 16, 128), jnp.bfloat16),
            pltpu.VMEM((256, 2048), jnp.bfloat16),
            pltpu.VMEM((256, 2048), jnp.bfloat16),
            pltpu.VMEM((TURNS, 256, 256), jnp.float32),
            dma,
            dma,
            dma,
            dma,
            dma,
            dma,
            dma,
            dma((2, 4, TURNS)),
            dma((2, 4, TURNS)),
            dma((TURNS,)),
            dma((TURNS,)),
            dma,
            dma,
            dma((TURNS,)),
            dma((TURNS,)),
            dma,
        ],
        compiler_params=pltpu.CompilerParams(collective_id=0, has_side_effects=True, vmem_limit_bytes=32 << 20),
    )(owner_order, dictionary, residual, coefs, pixel_of)


def maps_kernel(values, pixels, maps, select, parts, state):
    half = 2048

    def spread(q, _):
        points = pl.ds(pl.multiple_of(q * 256, 256), 256)
        ids = pixels[q]
        column = jnp.broadcast_to(ids, (8, 256)).T[:, 0:1] % half
        lane = lax.broadcasted_iota(jnp.int32, (256, 128), 1)
        one = jnp.where(column % 128 == lane, 1.0, 0.0).astype(jnp.bfloat16)
        block = jnp.broadcast_to(column // 128, (256, 128)).astype(jnp.float32).astype(jnp.bfloat16)
        for a in range(16):
            select[points, 128 * a : 128 * (a + 1)] = jnp.where(block == jnp.bfloat16(a), one, jnp.bfloat16(0))
        upper = ids >= half
        for t in range(TURNS):
            v = values[t, :, points]
            high = v.astype(jnp.bfloat16).astype(jnp.float32)
            rest = v - high
            for s, part in enumerate((high, rest)):
                lower_part = jnp.where(upper, 0.0, part).astype(jnp.bfloat16)
                upper_part = jnp.where(upper, part, 0.0).astype(jnp.bfloat16)
                parts[64 * s + 16 * t : 64 * s + 16 * t + 16, points] = lower_part
                parts[128 + 64 * s + 16 * t : 128 + 64 * s + 16 * t + 16, points] = upper_part
        return _

    lax.fori_loop(0, 16, spread, 0)
    for n in range(8):
        cols = slice(256 * n, 256 * (n + 1))
        placed = jnp.dot(parts[...], select[:, cols], preferred_element_type=jnp.float32)
        for h in range(2):
            whole = placed[128 * h : 128 * h + 64] + placed[128 * h + 64 : 128 * h + 128]
            for r in range(2):
                state[16 * h + 2 * n + r] = whole[:, 128 * r : 128 * (r + 1)]

    last = lax.broadcasted_iota(jnp.int32, (32, 8, 128), 2) == 127

    def flow(d):
        scaled = d / edge_scale
        return d / (1.0 + scaled * scaled)

    def smooth(group, _):
        rows = pl.ds(pl.multiple_of(group * 8, 8), 8)
        u = state[:, rows, :]
        for repeat in range(SWEEPS):
            right = jnp.where(last, 0.0, flow(pltpu.roll(u, 127, 2) - u))
            down = flow(u[1:] - u[:-1])
            none = jnp.zeros((1, 8, 128), jnp.float32)
            total = (right - pltpu.roll(right, 1, 2)) + (
                jnp.concatenate([down, none], axis=0) - jnp.concatenate([none, down], axis=0)
            )
            u = u + time_step * total
        for i in range(32):
            maps[rows, i, :] = u[i]
        return _

    lax.fori_loop(0, 8, smooth, 0)


def make_maps(values, pixels):
    vmem = pl.BlockSpec(memory_space=pltpu.VMEM)
    return pl.pallas_call(
        maps_kernel,
        name="make_maps",
        out_shape=jax.ShapeDtypeStruct((64, 32, 128), jnp.float32),
        in_specs=[vmem, vmem],
        out_specs=vmem,
        scratch_shapes=[
            pltpu.VMEM((4096, 2048), jnp.bfloat16),
            pltpu.VMEM((256, 4096), jnp.bfloat16),
            pltpu.VMEM((32, 64, 128), jnp.float32),
        ],
        compiler_params=pltpu.CompilerParams(vmem_limit_bytes=48 << 20),
    )(values, pixels)


def per_device(residual_in, coefs_in, dictionary, owner_order, pixel_of):
    coefs = coefs_in[0].transpose(1, 2, 0)
    values, pixels = unmix(owner_order, dictionary, residual_in[0], coefs, pixel_of)
    return make_maps(values, pixels).reshape(1, TURNS, 16, 32, MAP_W)


def solution(mesh):
    placed = (
        P("field", "point", None),
        P("field", "point", None, None),
        P("field", None),
        P(),
        P("field", "point"),
    )
    return jax.shard_map(
        per_device,
        mesh=mesh,
        in_specs=placed,
        out_specs=P("field", None, "point", None, None),
        check_vma=False,
    )
```

time: 183 us -> 115 us (0.63)
  the two profiles are of different devices: /device:TPU:2 before, /device:TPU:1 now
where the time goes in v2:
time: 115 us; the launch traced here: 114 us
  Pallas kernels  111 us (97%)
  local copies, waits for them, and re-layouts  3.29 us (3%)
    pallas_call x1, Pallas kernels, unmix(): pl.pallas_call(unmix_kernel, name='unmix', out_shape=(jax.ShapeDtypeStruc...  93.2 us
    pallas_call x1, Pallas kernels, make_maps(): pl.pallas_call(maps_kernel, name='make_maps', out_shape=jax.ShapeDtypeStr...  17.9 us
    unnamed x9, local copies, waits for them, and re-layouts  3.29 us

profile of v2, /device:TPU:1, one launch (start us, length us, event | category | flops | bytes accessed | tf_op | source)
XLA Modules:
  0.0 114.4 jit_solution(9188918401362528718)
XLA Ops:
  0.0 0.0 copy-start
  0.0 1.4 %copy.6 = bf16[1,256,4,256]{1,3,2,0:T(8,128)(2,1)S(1)} copy(bf16[1,256,4,256]{3,2,1,0:T(4,128)(2,1)} %param.6) | data formatting | bytes 1048576 | tf_op args[1]
  1.4 0.0 copy-start.2
  1.4 0.0 copy-start.3
  1.4 0.0 copy-done
  1.4 0.6 copy-done.2
  2.1 0.0 copy-done.3
  2.1 0.0 copy-start.1
  2.1 1.2 %copy-done.1 = bf16[1,256,2048]{2,1,0:T(8,128)(2,1)S(1)} copy-done((bf16[1,256,2048]{2,1,0:T(8,128)(2,1)S(1)}, bf16[1,256,2048]{2,1,0:T(8,128)(2,1)}, u32[]{:S(2)}) %copy-start.1) | copy-done | bytes 1048600
  3.3 93.2 %unmix.1 = (f32[4,16,4096]{2,1,0:T(8,128)S(1)}, s32[16,1,256]{2,1,0:T(1,128)S(1)}) custom-call(s32[32]{0:T(128)S(1)} %copy-done.3, bf16[256,2048]{1,0:T(8,128)(2,1)S(1)} %copy-done, bf16[256,2048]{1,0:T(8,128)(2,1)S(1)} %bitcast.6, bf16[4,256,256]{2,1,0:T(8,128)(2,1)S(1)} %bitcast.5, s32[1,256]{1,0:T(1,128)S(1)} %copy-done.2), custom_call_target="tpu_custom_call" | custom-call | tf_op jit(solution)/shard_map/unmix/pallas_call | solution.py:314
  96.5 17.9 %make_maps.1 = f32[64,32,128]{2,1,0:T(8,128)} custom-call(f32[4,16,4096]{2,1,0:T(8,128)S(1)} %get-tuple-element.7.values, s32[16,1,256]{2,1,0:T(1,128)S(1)} %get-tuple-element.8.pixels), custom_call_target="tpu_custom_call" | custom-call | tf_op jit(solution)/shard_map/make_maps/pallas_call | solution.py:409
Async XLA Ops:
  0.0 1.4 %copy-start = (bf16[256,2048]{1,0:T(8,128)(2,1)S(1)}, bf16[256,2048]{1,0:T(8,128)(2,1)}, u32[]{:S(2)}) copy-start(bf16[256,2048]{1,0:T(8,128)(2,1)} %block.1) | copy-start | bytes 3145732
  1.4 0.7 copy-start.2
  1.4 0.7 copy-start.3
  2.1 1.2 %copy-start.1 = (bf16[1,256,2048]{2,1,0:T(8,128)(2,1)S(1)}, bf16[1,256,2048]{2,1,0:T(8,128)(2,1)}, u32[]{:S(2)}) copy-start(bf16[1,256,2048]{2,1,0:T(8,128)(2,1)} %param.5) | copy-start | bytes 3145732

commit v3 on v2

--- a/solution.py
+++ b/solution.py
@@ -31,23 +31,29 @@
 
 
 def unmix_kernel(
-    owner,
+    owner_hbm,
     block,
     residual_hbm,
-    coefs,
+    coefs_hbm,
     pixel_of,
+    maps,
+    owner,
     values,
     pixels,
+    coefs_in,
+    coefs,
     g,
     cand,
     residual,
     templates,
     updated,
+    select,
+    parts,
+    state,
     a_send,
     a_recv,
     b_send,
     b_recv,
-    own_sem,
     z_send,
     z_recv,
     ring_send,
@@ -58,7 +64,7 @@
     id_recv,
     v_send,
     v_recv,
-    r_sem,
+    load_sem,
 ):
     f = lax.axis_index("field")
     p = lax.axis_index("point")
@@ -70,8 +76,6 @@
     z = zh * 4 + p % 4
     sibling = (f + 1 - 2 * core, p)
 
-    fetch = pltpu.make_async_copy(residual_hbm, residual, r_sem)
-    fetch.start()
     barrier = pltpu.get_barrier_semaphore()
 
     def greet(device):
@@ -103,29 +107,41 @@
 
     lax.fori_loop(1, 16, greet_point, 0)
     greet(sibling)
-    pl.semaphore_wait(barrier, 15 + 12 + 12 + 1)
-
     lanes = pl.ds(pl.multiple_of(p * 128, 128), 128)
 
     def tile_of(to):
         return block.at[pl.ds(pl.multiple_of(to * 16, 16), 16), lanes]
 
+    load_own = pltpu.make_async_copy(tile_of(chip), cand.at[core, chip], load_sem.at[0])
+    load_owner = pltpu.make_async_copy(owner_hbm, owner, load_sem.at[1])
+    load_pixels = pltpu.make_async_copy(pixel_of, pixels.at[p], load_sem.at[2])
+    load_coefs = pltpu.make_async_copy(coefs_hbm, coefs_in, load_sem.at[3])
+    load_residual = pltpu.make_async_copy(residual_hbm, residual, load_sem.at[4])
+    load_own.start()
+    load_owner.start()
+    load_pixels.start()
+    load_coefs.start()
+    load_residual.start()
+    pl.semaphore_wait(barrier, 15 + 12 + 12 + 1)
+
     def scatter(i, _):
-        to = (chip + i) % 16
-        remote(tile_of(to), cand.at[core, chip], a_send, a_recv, (to * 2 + core, p)).start()
-        return _
-
-    lax.fori_loop(1, 16, scatter, 0)
+        to = (chip + 4 * ((i // 4 + 2) % 4) + i % 4) % 16
+
+        @pl.when(to != chip)
+        def _send():
+            remote(tile_of(to), cand.at[core, chip], a_send, a_recv, (to * 2 + core, p)).start()
+
+        return _
+
+    lax.fori_loop(0, 16, scatter, 0)
 
     def tell_pixels(i, _):
         remote(pixel_of, pixels.at[p], id_send, id_recv, (f, (p + i) % 16)).start()
         return _
 
     lax.fori_loop(1, 16, tell_pixels, 0)
-    pixels[p] = pixel_of[...]
-    own = pltpu.make_async_copy(tile_of(chip), cand.at[core, chip], own_sem)
-    own.start()
-    own.wait()
+    load_own.wait()
+    load_owner.wait()
     all_a = remote(cand.at[0, pl.ds(0, 15)], cand.at[0, pl.ds(0, 15)], a_send, a_recv, sibling)
     all_a.wait_recv()
     both = remote(cand.at[core], cand.at[core], b_send, b_recv, sibling)
@@ -140,10 +156,14 @@
 
     def along_z(i, _):
         part = g.at[core, :, p, zh, mine, :]
-        remote(part, part, z_send, z_recv, dev((z + i) % 16, x, core, y)).start()
-        return _
-
-    lax.fori_loop(1, 16, along_z, 0)
+        step = 8 + (i + 1) // 2 * (1 - i % 2 * 2)
+        remote(part, part, z_send, z_recv, dev((z + step) % 16, x, core, y)).start()
+        return _
+
+    lax.fori_loop(0, 15, along_z, 0)
+    load_coefs.wait()
+    for t in range(TURNS):
+        coefs[t] = coefs_in[:, t, :].astype(jnp.float32).T
     amount = g.at[0, 0, pl.ds(0, 15), 0, pl.ds(0, 32), :]
     all_z = remote(amount, amount, z_send, z_recv, sibling)
     all_z.wait_recv()
@@ -221,28 +241,36 @@
         def _odd():
             act(*rings("x", "y"))
 
-    def open_rings(mid, last):
+    def open_mid(mid, last):
         for t in range(TURNS):
             mid[0](t)
+
+    def pass_mid(mid, last):
         for t in range(TURNS):
             mid[1](t)
+
+    def open_last(mid, last):
+        for t in range(TURNS):
             mid[2](t)
             last[0](t)
 
+    def share(last, t):
+        last[2](t)
+        swap(t).start()
+
     def first_half(mid, last):
-        for t in (0, 1):
-            last[1](t)
-            last[2](t)
-            swap(t).start()
+        last[1](0)
+        last[1](1)
+        share(last, 0)
+        last[1](2)
+        share(last, 1)
 
     def middle(mid, last):
-        last[1](2)
+        last[1](3)
+        share(last, 2)
 
     def second_half(mid, last):
-        last[1](3)
-        for t in (2, 3):
-            last[2](t)
-            swap(t).start()
+        share(last, 3)
 
     def close(mid, last):
         for t in range(TURNS):
@@ -259,7 +287,7 @@
             templates[:, 128 * q : 128 * (q + 1)] = g[t % 2, t // 2, q].reshape(256, 128)
         gram = nt(templates[...], templates[...])
         step = 1.0 / jnp.sum(jnp.abs(gram), axis=1, keepdims=True)
-        before = coefs[t].astype(jnp.float32)
+        before = coefs[t]
         after = jnp.maximum(before + step * nt(templates[...], residual[...]), 0.0)
         updated[t] = after
 
@@ -281,112 +309,51 @@
                 )
                 residual[:, cols] = (residual[:, cols].astype(jnp.float32) - moved).astype(jnp.bfloat16)
 
-    by_core(open_rings)
-    fetch.wait()
-    by_core(first_half)
-    swap(0).wait_recv()
-    swap(1).wait_recv()
-    turn(0)
-    by_core(middle)
-    turn(1)
-    by_core(second_half)
-    swap(2).wait_recv()
-    swap(3).wait_recv()
-    turn(2)
-    turn(3)
-    by_core(close)
-    for t in range(TURNS):
-        swap(t).wait_send()
-    ids = remote(pixels.at[pl.ds(0, 15)], pixels.at[pl.ds(0, 15)], id_send, id_recv, sibling)
-    ids.wait_send()
-    ids.wait_recv()
-    for t in range(TURNS):
-        amount = values.at[t, :, pl.ds(0, 15 * 256)]
-        done = remote(amount, amount, v_send.at[t], v_recv.at[t], sibling)
-        done.wait_send()
-        done.wait_recv()
-
-
-def unmix(owner_order, dictionary, residual, coefs, pixel_of):
-    vmem = pl.BlockSpec(memory_space=pltpu.VMEM)
-    hbm = pl.BlockSpec(memory_space=pl.ANY)
-    dma = pltpu.SemaphoreType.DMA
-    return pl.pallas_call(
-        unmix_kernel,
-        name="unmix",
-        out_shape=(
-            jax.ShapeDtypeStruct((TURNS, 16, 4096), jnp.float32),
-            jax.ShapeDtypeStruct((16, 1, 256), jnp.int32),
-        ),
-        in_specs=[pl.BlockSpec(memory_space=pltpu.SMEM), hbm, hbm, vmem, vmem],
-        out_specs=(vmem, vmem),
-        scratch_shapes=[
-            pltpu.VMEM((2, 2, 16, 4, 64, 128), jnp.bfloat16),
-            pltpu.VMEM((2, 16, 16, 128), jnp.bfloat16),
-            pltpu.VMEM((256, 2048), jnp.bfloat16),
-            pltpu.VMEM((256, 2048), jnp.bfloat16),
-            pltpu.VMEM((TURNS, 256, 256), jnp.float32),
-            dma,
-            dma,
-            dma,
-            dma,
-            dma,
-            dma,
-            dma,
-            dma((2, 4, TURNS)),
-            dma((2, 4, TURNS)),
-            dma((TURNS,)),
-            dma((TURNS,)),
-            dma,
-            dma,
-            dma((TURNS,)),
-            dma((TURNS,)),
-            dma,
-        ],
-        compiler_params=pltpu.CompilerParams(collective_id=0, has_side_effects=True, vmem_limit_bytes=32 << 20),
-    )(owner_order, dictionary, residual, coefs, pixel_of)
-
-
-def maps_kernel(values, pixels, maps, select, parts, state):
     half = 2048
 
     def spread(q, _):
         points = pl.ds(pl.multiple_of(q * 256, 256), 256)
-        ids = pixels[q]
-        column = jnp.broadcast_to(ids, (8, 256)).T[:, 0:1] % half
+        column = jnp.broadcast_to(pixels[q], (8, 256)).T[:, 0:1] % half
         lane = lax.broadcasted_iota(jnp.int32, (256, 128), 1)
         one = jnp.where(column % 128 == lane, 1.0, 0.0).astype(jnp.bfloat16)
-        block = jnp.broadcast_to(column // 128, (256, 128)).astype(jnp.float32).astype(jnp.bfloat16)
+        group = jnp.broadcast_to(column // 128, (256, 128)).astype(jnp.float32).astype(jnp.bfloat16)
         for a in range(16):
-            select[points, 128 * a : 128 * (a + 1)] = jnp.where(block == jnp.bfloat16(a), one, jnp.bfloat16(0))
-        upper = ids >= half
-        for t in range(TURNS):
-            v = values[t, :, points]
-            high = v.astype(jnp.bfloat16).astype(jnp.float32)
-            rest = v - high
-            for s, part in enumerate((high, rest)):
-                lower_part = jnp.where(upper, 0.0, part).astype(jnp.bfloat16)
-                upper_part = jnp.where(upper, part, 0.0).astype(jnp.bfloat16)
-                parts[64 * s + 16 * t : 64 * s + 16 * t + 16, points] = lower_part
-                parts[128 + 64 * s + 16 * t : 128 + 64 * s + 16 * t + 16, points] = upper_part
-        return _
-
-    lax.fori_loop(0, 16, spread, 0)
-    for n in range(8):
-        cols = slice(256 * n, 256 * (n + 1))
-        placed = jnp.dot(parts[...], select[:, cols], preferred_element_type=jnp.float32)
-        for h in range(2):
-            whole = placed[128 * h : 128 * h + 64] + placed[128 * h + 64 : 128 * h + 128]
-            for r in range(2):
-                state[16 * h + 2 * n + r] = whole[:, 128 * r : 128 * (r + 1)]
-
-    last = lax.broadcasted_iota(jnp.int32, (32, 8, 128), 2) == 127
+            select[points, 128 * a : 128 * (a + 1)] = jnp.where(group == jnp.bfloat16(a), one, jnp.bfloat16(0))
+        return _
+
+    def split(pair):
+        def one(q, _):
+            points = pl.ds(pl.multiple_of(q * 256, 256), 256)
+            upper = pixels[q] >= half
+            for i in range(2):
+                v = values[2 * pair + i, :, points]
+                high = v.astype(jnp.bfloat16).astype(jnp.float32)
+                for s, part in enumerate((high, v - high)):
+                    row = 32 * s + 16 * i
+                    parts[row : row + 16, points] = jnp.where(upper, 0.0, part).astype(jnp.bfloat16)
+                    parts[64 + row : 64 + row + 16, points] = jnp.where(upper, part, 0.0).astype(jnp.bfloat16)
+            return _
+
+        lax.fori_loop(0, 16, one, 0)
+
+    def place(pair):
+        def one(n, _):
+            cols = pl.ds(pl.multiple_of(n * 256, 256), 256)
+            placed = jnp.dot(parts[...], select[:, cols], preferred_element_type=jnp.float32)
+            for h in range(2):
+                whole = placed[64 * h : 64 * h + 32] + placed[64 * h + 32 : 64 * h + 64]
+                for r in range(2):
+                    state[16 * h + 2 * n + r, 32 * pair : 32 * pair + 32] = whole[:, 128 * r : 128 * (r + 1)]
+            return _
+
+        lax.fori_loop(0, 8, one, 0)
 
     def flow(d):
         scaled = d / edge_scale
         return d / (1.0 + scaled * scaled)
 
     def smooth(group, _):
+        last = lax.broadcasted_iota(jnp.int32, (32, 8, 128), 2) == 127
         rows = pl.ds(pl.multiple_of(group * 8, 8), 8)
         u = state[:, rows, :]
         for repeat in range(SWEEPS):
@@ -401,30 +368,92 @@
             maps[rows, i, :] = u[i]
         return _
 
-    lax.fori_loop(0, 8, smooth, 0)
-
-
-def make_maps(values, pixels):
-    vmem = pl.BlockSpec(memory_space=pltpu.VMEM)
+    by_core(open_mid)
+    ids = remote(pixels.at[pl.ds(0, 15)], pixels.at[pl.ds(0, 15)], id_send, id_recv, sibling)
+    load_pixels.wait()
+    ids.wait_recv()
+    lax.fori_loop(0, 4, spread, 0)
+    by_core(pass_mid)
+    lax.fori_loop(4, 8, spread, 0)
+    by_core(open_last)
+    lax.fori_loop(8, 16, spread, 0)
+    load_residual.wait()
+    by_core(first_half)
+    swap(0).wait_recv()
+    swap(1).wait_recv()
+    turn(0)
+    by_core(middle)
+    turn(1)
+    by_core(second_half)
+    swap(2).wait_recv()
+    swap(3).wait_recv()
+    turn(2)
+    turn(3)
+
+    def arrived(t):
+        amount = values.at[t, :, pl.ds(0, 15 * 256)]
+        remote(amount, amount, v_send.at[t], v_recv.at[t], sibling).wait_recv()
+
+    for pair in range(2):
+        arrived(2 * pair)
+        arrived(2 * pair + 1)
+        split(pair)
+        place(pair)
+        lax.fori_loop(4 * pair, 4 * pair + 4, smooth, 0)
+    by_core(close)
+    ids.wait_send()
+    for t in range(TURNS):
+        swap(t).wait_send()
+        amount = values.at[t, :, pl.ds(0, 15 * 256)]
+        remote(amount, amount, v_send.at[t], v_recv.at[t], sibling).wait_send()
+
+
+def unmix(owner_order, dictionary, residual, coefs, pixel_of):
+    hbm = pl.BlockSpec(memory_space=pltpu.HBM)
+    dma = pltpu.SemaphoreType.DMA
     return pl.pallas_call(
-        maps_kernel,
-        name="make_maps",
+        unmix_kernel,
+        name="unmix",
         out_shape=jax.ShapeDtypeStruct((64, 32, 128), jnp.float32),
-        in_specs=[vmem, vmem],
-        out_specs=vmem,
+        in_specs=[hbm] * 5,
+        out_specs=pl.BlockSpec(memory_space=pltpu.VMEM),
         scratch_shapes=[
+            pltpu.SMEM((32,), jnp.int32),
+            pltpu.VMEM((TURNS, 16, 4096), jnp.float32),
+            pltpu.VMEM((16, 1, 256), jnp.int32),
+            pltpu.VMEM((256, TURNS, 256), jnp.bfloat16),
+            pltpu.VMEM((TURNS, 256, 256), jnp.float32),
+            pltpu.VMEM((2, 2, 16, 4, 64, 128), jnp.bfloat16),
+            pltpu.VMEM((2, 16, 16, 128), jnp.bfloat16),
+            pltpu.VMEM((256, 2048), jnp.bfloat16),
+            pltpu.VMEM((256, 2048), jnp.bfloat16),
+            pltpu.VMEM((TURNS, 256, 256), jnp.float32),
             pltpu.VMEM((4096, 2048), jnp.bfloat16),
-            pltpu.VMEM((256, 4096), jnp.bfloat16),
+            pltpu.VMEM((128, 4096), jnp.bfloat16),
             pltpu.VMEM((32, 64, 128), jnp.float32),
+            dma,
+            dma,
+            dma,
+            dma,
+            dma,
+            dma,
+            dma((2, 4, TURNS)),
+            dma((2, 4, TURNS)),
+            dma((TURNS,)),
+            dma((TURNS,)),
+            dma,
+            dma,
+            dma((TURNS,)),
+            dma((TURNS,)),
+            dma((5,)),
         ],
-        compiler_params=pltpu.CompilerParams(vmem_limit_bytes=48 << 20),
-    )(values, pixels)
+        compiler_params=pltpu.CompilerParams(collective_id=0, has_side_effects=True, vmem_limit_bytes=48 << 20),
+    )(owner_order, dictionary, residual, coefs, pixel_of)
 
 
 def per_device(residual_in, coefs_in, dictionary, owner_order, pixel_of):
-    coefs = coefs_in[0].transpose(1, 2, 0)
-    values, pixels = unmix(owner_order, dictionary, residual_in[0], coefs, pixel_of)
-    return make_maps(values, pixels).reshape(1, TURNS, 16, 32, MAP_W)
+    maps = unmix(owner_order, dictionary, residual_in[0], coefs_in[0], pixel_of)
+    return maps.reshape(1, TURNS, 16, 32, MAP_W)
 
 
 def solution(mesh):

time: 115 us -> 96.6 us (0.84)
  Pallas kernels: 111 us -> 91.2 us
  local copies, waits for them, and re-layouts: 3.29 us -> 5.14 us
    pallas_call x2 -> x1, Pallas kernels: 111 us -> 91.2 us  [unmix(): pl.pallas_call(unmix_kernel, name='unmix', out_shape=jax.ShapeDtypeStruct...]
    unnamed x9 -> x11, local copies, waits for them, and re-layouts: 3.29 us -> 5.14 us
where the time goes in v3:
time: 96.6 us; the launch traced here: 96.4 us
  Pallas kernels  91.2 us (94%)
  local copies, waits for them, and re-layouts  5.14 us (5%)
    pallas_call x1, Pallas kernels, unmix(): pl.pallas_call(unmix_kernel, name='unmix', out_shape=jax.ShapeDtypeStruct...  91.2 us
    unnamed x11, local copies, waits for them, and re-layouts  5.14 us

profile of v3, /device:TPU:1, one launch (start us, length us, event | category | flops | bytes accessed | tf_op | source)
XLA Modules:
  0.0 96.4 jit_solution(17126240115748044213)
XLA Ops:
  0.0 0.0 copy-start.3
  0.0 0.0 copy-start.4
  0.0 0.7 copy-done.3
  0.7 0.0 copy-done.4
  0.7 0.0 copy-start
  0.7 1.2 %copy-done = bf16[256,2048]{1,0:T(8,128)(2,1)S(1)} copy-done((bf16[256,2048]{1,0:T(8,128)(2,1)S(1)}, bf16[256,2048]{1,0:T(8,128)(2,1)}, u32[]{:S(2)}) %copy-start) | copy-done | bytes 1048600
  1.9 0.0 copy-start.1
  1.9 1.2 %copy-done.1 = bf16[1,256,2048]{2,1,0:T(8,128)(2,1)S(1)} copy-done((bf16[1,256,2048]{2,1,0:T(8,128)(2,1)S(1)}, bf16[1,256,2048]{2,1,0:T(8,128)(2,1)}, u32[]{:S(2)}) %copy-start.1) | copy-done | bytes 1048600
  3.1 0.0 copy-start.2
  3.1 1.0 %copy-done.2 = bf16[1,256,4,256]{3,2,1,0:T(4,128)(2,1)S(1)} copy-done((bf16[1,256,4,256]{3,2,1,0:T(4,128)(2,1)S(1)}, bf16[1,256,4,256]{3,2,1,0:T(4,128)(2,1)}, u32[]{:S(2)}) %copy-start.2) | copy-done | bytes 524312
  4.2 91.2 %unmix.1 = f32[64,32,128]{2,1,0:T(8,128)S(1)} custom-call(s32[32]{0:T(128)S(1)} %copy-done.4, bf16[256,2048]{1,0:T(8,128)(2,1)S(1)} %copy-done, bf16[256,2048]{1,0:T(8,128)(2,1)S(1)} %bitcast.4, bf16[256,4,256]{2,1,0:T(4,128)(2,1)S(1)} %bitcast.5, s32[1,256]{1,0:T(1,128)S(1)} %copy-done.3), custom_call_target="tpu_custom_call" | custom-call | tf_op jit(solution)/shard_map/unmix/pallas_call | solution.py:414
  95.4 1.0 %copy.7 = f32[1,4,16,32,128]{4,3,2,1,0:T(8,128)} copy(f32[1,4,16,32,128]{4,3,2,1,0:T(8,128)S(1)} %bitcast.3) | data formatting | bytes 2097152
Async XLA Ops:
  0.0 0.7 copy-start.3
  0.0 0.7 copy-start.4
  0.7 1.2 %copy-start = (bf16[256,2048]{1,0:T(8,128)(2,1)S(1)}, bf16[256,2048]{1,0:T(8,128)(2,1)}, u32[]{:S(2)}) copy-start(bf16[256,2048]{1,0:T(8,128)(2,1)} %block.1) | copy-start | bytes 3145732
  1.9 1.2 %copy-start.1 = (bf16[1,256,2048]{2,1,0:T(8,128)(2,1)S(1)}, bf16[1,256,2048]{2,1,0:T(8,128)(2,1)}, u32[]{:S(2)}) copy-start(bf16[1,256,2048]{2,1,0:T(8,128)(2,1)} %param.5) | copy-start | bytes 3145732
  3.1 1.0 %copy-start.2 = (bf16[1,256,4,256]{3,2,1,0:T(4,128)(2,1)S(1)}, bf16[1,256,4,256]{3,2,1,0:T(4,128)(2,1)}, u32[]{:S(2)}) copy-start(bf16[1,256,4,256]{3,2,1,0:T(4,128)(2,1)} %param.6) | copy-start | bytes 1572868

commit v4 on v3

--- a/solution.py
+++ b/solution.py
@@ -11,6 +11,7 @@
 SWEEPS = 4
 MAP_W = 128
 MESH = pl.DeviceIdType.MESH
+LEVELS = 65534.0
 
 time_step = 0.2
 edge_scale = 0.5
@@ -38,7 +39,9 @@
     pixel_of,
     maps,
     owner,
-    values,
+    codes,
+    peaks,
+    peak_cols,
     pixels,
     coefs_in,
     coefs,
@@ -64,6 +67,8 @@
     id_recv,
     v_send,
     v_recv,
+    s_send,
+    s_recv,
     load_sem,
 ):
     f = lax.axis_index("field")
@@ -280,7 +285,7 @@
     def send_rows(t, to):
         rows = pl.ds(pl.multiple_of(to * 16, 16), 16)
         points = pl.ds(pl.multiple_of(p * 256, 256), 256)
-        return updated.at[t, rows], values.at[t, :, points]
+        return updated.at[t, rows], codes.at[t, :, points]
 
     def turn(t):
         for q in range(16):
@@ -289,17 +294,21 @@
         step = 1.0 / jnp.sum(jnp.abs(gram), axis=1, keepdims=True)
         before = coefs[t]
         after = jnp.maximum(before + step * nt(templates[...], residual[...]), 0.0)
-        updated[t] = after
+        peak = jnp.max(after, axis=1, keepdims=True)
+        share_of_peak = after / jnp.where(peak > 0.0, peak, 1.0)
+        updated[t] = (jnp.floor(share_of_peak * LEVELS + 0.5) - LEVELS / 2).astype(jnp.int32).astype(jnp.int16)
+        peaks[t, p] = jnp.broadcast_to(peak, (256, 128)).T[0:1]
 
         def deliver(i, _):
             to = (p + i) % 16
             src, dst = send_rows(t, to)
             remote(src, dst, v_send.at[t], v_recv.at[t], (f, to)).start()
+            remote(peaks.at[t, p], peaks.at[t, p], s_send.at[t], s_recv.at[t], (f, to)).start()
             return _
 
         lax.fori_loop(1, 16, deliver, 0)
         rows = pl.ds(pl.multiple_of(p * 16, 16), 16)
-        values[t, :, pl.ds(pl.multiple_of(p * 256, 256), 256)] = updated[t, rows, :]
+        codes[t, :, pl.ds(pl.multiple_of(p * 256, 256), 256)] = updated[t, rows, :]
         if t + 1 < TURNS:
             change = (after - before).astype(jnp.bfloat16)
             for q in range(4):
@@ -321,17 +330,21 @@
             select[points, 128 * a : 128 * (a + 1)] = jnp.where(group == jnp.bfloat16(a), one, jnp.bfloat16(0))
         return _
 
-    def split(pair):
+    def split(t):
+        peak_cols[:, 0:16] = peaks[t].reshape(16, 256).T
+        own_peaks = peak_cols[pl.ds(pl.multiple_of(p * 16, 16), 16), :] * (1.0 / LEVELS)
+        source = lax.broadcasted_iota(jnp.int32, (16, 128), 1)
+
         def one(q, _):
             points = pl.ds(pl.multiple_of(q * 256, 256), 256)
             upper = pixels[q] >= half
-            for i in range(2):
-                v = values[2 * pair + i, :, points]
-                high = v.astype(jnp.bfloat16).astype(jnp.float32)
-                for s, part in enumerate((high, v - high)):
-                    row = 32 * s + 16 * i
-                    parts[row : row + 16, points] = jnp.where(upper, 0.0, part).astype(jnp.bfloat16)
-                    parts[64 + row : 64 + row + 16, points] = jnp.where(upper, part, 0.0).astype(jnp.bfloat16)
+            scale = jnp.sum(jnp.where(source == q, own_peaks, 0.0), axis=1, keepdims=True)
+            v = (codes[t, :, points].astype(jnp.int32).astype(jnp.float32) + LEVELS / 2) * scale
+            high = v.astype(jnp.bfloat16).astype(jnp.float32)
+            for s, part in enumerate((high, v - high)):
+                row = 32 * s + t % 2 * 16
+                parts[row : row + 16, points] = jnp.where(upper, 0.0, part).astype(jnp.bfloat16)
+                parts[64 + row : 64 + row + 16, points] = jnp.where(upper, part, 0.0).astype(jnp.bfloat16)
             return _
 
         lax.fori_loop(0, 16, one, 0)
@@ -349,7 +362,7 @@
         lax.fori_loop(0, 8, one, 0)
 
     def flow(d):
-        scaled = d / edge_scale
+        scaled = d * (1.0 / edge_scale)
         return d / (1.0 + scaled * scaled)
 
     def smooth(group, _):
@@ -390,22 +403,27 @@
     turn(2)
     turn(3)
 
-    def arrived(t):
-        amount = values.at[t, :, pl.ds(0, 15 * 256)]
-        remote(amount, amount, v_send.at[t], v_recv.at[t], sibling).wait_recv()
+    def sent(t):
+        amount = codes.at[t, :, pl.ds(0, 15 * 256)]
+        rows = peaks.at[t, pl.ds(0, 15)]
+        return (
+            remote(amount, amount, v_send.at[t], v_recv.at[t], sibling),
+            remote(rows, rows, s_send.at[t], s_recv.at[t], sibling),
+        )
 
     for pair in range(2):
-        arrived(2 * pair)
-        arrived(2 * pair + 1)
-        split(pair)
+        for t in (2 * pair, 2 * pair + 1):
+            for copies in sent(t):
+                copies.wait_recv()
+            split(t)
         place(pair)
         lax.fori_loop(4 * pair, 4 * pair + 4, smooth, 0)
     by_core(close)
     ids.wait_send()
     for t in range(TURNS):
         swap(t).wait_send()
-        amount = values.at[t, :, pl.ds(0, 15 * 256)]
-        remote(amount, amount, v_send.at[t], v_recv.at[t], sibling).wait_send()
+        for copies in sent(t):
+            copies.wait_send()
 
 
 def unmix(owner_order, dictionary, residual, coefs, pixel_of):
@@ -419,7 +437,9 @@
         out_specs=pl.BlockSpec(memory_space=pltpu.VMEM),
         scratch_shapes=[
             pltpu.SMEM((32,), jnp.int32),
-            pltpu.VMEM((TURNS, 16, 4096), jnp.float32),
+            pltpu.VMEM((TURNS, 16, 4096), jnp.int16),
+            pltpu.VMEM((TURNS, 16, 1, 256), jnp.float32),
+            pltpu.VMEM((256, 128), jnp.float32),
             pltpu.VMEM((16, 1, 256), jnp.int32),
             pltpu.VMEM((256, TURNS, 256), jnp.bfloat16),
             pltpu.VMEM((TURNS, 256, 256), jnp.float32),
@@ -427,7 +447,7 @@
             pltpu.VMEM((2, 16, 16, 128), jnp.bfloat16),
             pltpu.VMEM((256, 2048), jnp.bfloat16),
             pltpu.VMEM((256, 2048), jnp.bfloat16),
-            pltpu.VMEM((TURNS, 256, 256), jnp.float32),
+            pltpu.VMEM((TURNS, 256, 256), jnp.int16),
             pltpu.VMEM((4096, 2048), jnp.bfloat16),
             pltpu.VMEM((128, 4096), jnp.bfloat16),
             pltpu.VMEM((32, 64, 128), jnp.float32),
@@ -445,9 +465,11 @@
             dma,
             dma((TURNS,)),
             dma((TURNS,)),
+            dma((TURNS,)),
+            dma((TURNS,)),
             dma((5,)),
         ],
-        compiler_params=pltpu.CompilerParams(collective_id=0, has_side_effects=True, vmem_limit_bytes=48 << 20),
+        compiler_params=pltpu.CompilerParams(collective_id=0, has_side_effects=True, vmem_limit_bytes=60 << 20),
     )(owner_order, dictionary, residual, coefs, pixel_of)
 
 

time: 96.6 us -> 91.2 us (0.944)
  local copies, waits for them, and re-layouts: 5.14 us -> 2.26 us
  Pallas kernels: 91.2 us -> 88.8 us
    unnamed x11 -> x1, local copies, waits for them, and re-layouts: 5.14 us -> 2.26 us
    pallas_call x1, Pallas kernels: 91.2 us -> 88.8 us  [unmix(): pl.pallas_call(unmix_kernel, name='unmix', out_shape=jax.ShapeDtypeStruct...]
where the time goes in v4:
time: 91.2 us; the launch traced here: 91.1 us
  Pallas kernels  88.8 us (97%)
  local copies, waits for them, and re-layouts  2.26 us (2%)
    pallas_call x1, Pallas kernels, unmix(): pl.pallas_call(unmix_kernel, name='unmix', out_shape=jax.ShapeDtypeStruct...  88.8 us
    unnamed x1, local copies, waits for them, and re-layouts  2.26 us

profile of v4, /device:TPU:1, one launch (start us, length us, event | category | flops | bytes accessed | tf_op | source)
XLA Modules:
  0.0 91.1 jit_solution(9699748601827225672)
XLA Ops:
  0.0 88.8 %unmix.1 = f32[64,32,128]{2,1,0:T(8,128)} custom-call(s32[32]{0:T(128)} %owner_hbm.1, bf16[256,2048]{1,0:T(8,128)(2,1)} %block.1, bf16[256,2048]{1,0:T(8,128)(2,1)} %bitcast.4, bf16[256,4,256]{2,1,0:T(4,128)(2,1)} %bitcast.5, s32[1,256]{1,0:T(1,128)} %pixel_of.1), custom_call_target="tpu_custom_call" | custom-call | tf_op jit(solution)/shard_map/unmix/pallas_call | solution.py:432
  88.8 2.3 %copy.7 = f32[1,4,16,32,128]{4,3,2,1,0:T(8,128)} copy(f32[1,4,16,32,128]{4,3,2,1,0:T(8,128)} %bitcast.3) | data formatting | bytes 2097152

commit v5 on v4

--- a/solution.py
+++ b/solution.py
@@ -12,6 +12,8 @@
 MAP_W = 128
 MESH = pl.DeviceIdType.MESH
 LEVELS = 65534.0
+GROUPS = 8
+SPAN = 4096 // GROUPS
 
 time_step = 0.2
 edge_scale = 0.5
@@ -50,6 +52,7 @@
     residual,
     templates,
     updated,
+    member,
     select,
     parts,
     state,
@@ -257,7 +260,8 @@
     def open_last(mid, last):
         for t in range(TURNS):
             mid[2](t)
-            last[0](t)
+            if t < 2:
+                last[0](t)
 
     def share(last, t):
         last[2](t)
@@ -265,7 +269,9 @@
 
     def first_half(mid, last):
         last[1](0)
+        last[0](2)
         last[1](1)
+        last[0](3)
         share(last, 0)
         last[1](2)
         share(last, 1)
@@ -318,16 +324,15 @@
                 )
                 residual[:, cols] = (residual[:, cols].astype(jnp.float32) - moved).astype(jnp.bfloat16)
 
-    half = 2048
-
     def spread(q, _):
         points = pl.ds(pl.multiple_of(q * 256, 256), 256)
-        column = jnp.broadcast_to(pixels[q], (8, 256)).T[:, 0:1] % half
-        lane = lax.broadcasted_iota(jnp.int32, (256, 128), 1)
-        one = jnp.where(column % 128 == lane, 1.0, 0.0).astype(jnp.bfloat16)
-        group = jnp.broadcast_to(column // 128, (256, 128)).astype(jnp.float32).astype(jnp.bfloat16)
-        for a in range(16):
-            select[points, 128 * a : 128 * (a + 1)] = jnp.where(group == jnp.bfloat16(a), one, jnp.bfloat16(0))
+        ids = pixels[q]
+        for h in range(GROUPS):
+            here = jnp.where(ids // SPAN == h, 1.0, 0.0)
+            member[16 * h : 16 * h + 16, points] = jnp.broadcast_to(here, (16, 256)).astype(jnp.bfloat16)
+        column = jnp.broadcast_to(ids, (8, 256)).T[:, 0:1] % SPAN
+        lane = lax.broadcasted_iota(jnp.int32, (256, SPAN), 1)
+        select[points, :] = jnp.where(column == lane, 1.0, 0.0).astype(jnp.bfloat16)
         return _
 
     def split(t):
@@ -337,29 +342,28 @@
 
         def one(q, _):
             points = pl.ds(pl.multiple_of(q * 256, 256), 256)
-            upper = pixels[q] >= half
             scale = jnp.sum(jnp.where(source == q, own_peaks, 0.0), axis=1, keepdims=True)
             v = (codes[t, :, points].astype(jnp.int32).astype(jnp.float32) + LEVELS / 2) * scale
-            high = v.astype(jnp.bfloat16).astype(jnp.float32)
-            for s, part in enumerate((high, v - high)):
-                row = 32 * s + t % 2 * 16
-                parts[row : row + 16, points] = jnp.where(upper, 0.0, part).astype(jnp.bfloat16)
-                parts[64 + row : 64 + row + 16, points] = jnp.where(upper, part, 0.0).astype(jnp.bfloat16)
+            high = v.astype(jnp.bfloat16)
+            rest = (v - high.astype(jnp.float32)).astype(jnp.bfloat16)
+            for h in range(GROUPS):
+                here = member[16 * h : 16 * h + 16, points]
+                parts[32 * h : 32 * h + 16, points] = high * here
+                parts[32 * h + 16 : 32 * h + 32, points] = rest * here
             return _
 
         lax.fori_loop(0, 16, one, 0)
 
-    def place(pair):
-        def one(n, _):
-            cols = pl.ds(pl.multiple_of(n * 256, 256), 256)
-            placed = jnp.dot(parts[...], select[:, cols], preferred_element_type=jnp.float32)
-            for h in range(2):
-                whole = placed[64 * h : 64 * h + 32] + placed[64 * h + 32 : 64 * h + 64]
+    def place(t):
+        for n in range(SPAN // 256):
+            placed = jnp.dot(
+                parts[...], select[:, 256 * n : 256 * (n + 1)], preferred_element_type=jnp.float32
+            )
+            for h in range(GROUPS):
+                whole = placed[32 * h : 32 * h + 16] + placed[32 * h + 16 : 32 * h + 32]
                 for r in range(2):
-                    state[16 * h + 2 * n + r, 32 * pair : 32 * pair + 32] = whole[:, 128 * r : 128 * (r + 1)]
-            return _
-
-        lax.fori_loop(0, 8, one, 0)
+                    row = h * (SPAN // 128) + 2 * n + r
+                    state[row, 16 * t : 16 * t + 16] = whole[:, 128 * r : 128 * (r + 1)]
 
     def flow(d):
         scaled = d * (1.0 / edge_scale)
@@ -411,13 +415,12 @@
             remote(rows, rows, s_send.at[t], s_recv.at[t], sibling),
         )
 
-    for pair in range(2):
-        for t in (2 * pair, 2 * pair + 1):
-            for copies in sent(t):
-                copies.wait_recv()
-            split(t)
-        place(pair)
-        lax.fori_loop(4 * pair, 4 * pair + 4, smooth, 0)
+    for t in range(TURNS):
+        for copies in sent(t):
+            copies.wait_recv()
+        split(t)
+        place(t)
+        lax.fori_loop(2 * t, 2 * t + 2, smooth, 0)
     by_core(close)
     ids.wait_send()
     for t in range(TURNS):
@@ -448,8 +451,9 @@
             pltpu.VMEM((256, 2048), jnp.bfloat16),
             pltpu.VMEM((256, 2048), jnp.bfloat16),
             pltpu.VMEM((TURNS, 256, 256), jnp.int16),
-            pltpu.VMEM((4096, 2048), jnp.bfloat16),
-            pltpu.VMEM((128, 4096), jnp.bfloat16),
+            pltpu.VMEM((16 * GROUPS, 4096), jnp.bfloat16),
+            pltpu.VMEM((4096, SPAN), jnp.bfloat16),
+            pltpu.VMEM((32 * GROUPS, 4096), jnp.bfloat16),
             pltpu.VMEM((32, 64, 128), jnp.float32),
             dma,
             dma,

time: 91.2 us -> 90.2 us (0.989)
  Pallas kernels: 88.8 us -> 87.3 us
    pallas_call x1, Pallas kernels: 88.8 us -> 87.3 us  [unmix(): pl.pallas_call(unmix_kernel, name='unmix', out_shape=jax.ShapeDtypeStruct...]
where the time goes in v5:
time: 90.2 us; the launch traced here: 89.5 us
  Pallas kernels  87.3 us (97%)
  local copies, waits for them, and re-layouts  2.26 us (3%)
    pallas_call x1, Pallas kernels, unmix(): pl.pallas_call(unmix_kernel, name='unmix', out_shape=jax.ShapeDtypeStruct...  87.3 us
    unnamed x1, local copies, waits for them, and re-layouts  2.26 us

profile of v5, /device:TPU:1, one launch (start us, length us, event | category | flops | bytes accessed | tf_op | source)
XLA Modules:
  0.0 89.5 jit_solution(6429581173259961194)
XLA Ops:
  0.0 87.3 %unmix.1 = f32[64,32,128]{2,1,0:T(8,128)} custom-call(s32[32]{0:T(128)} %owner_hbm.1, bf16[256,2048]{1,0:T(8,128)(2,1)} %block.1, bf16[256,2048]{1,0:T(8,128)(2,1)} %bitcast.4, bf16[256,4,256]{2,1,0:T(4,128)(2,1)} %bitcast.5, s32[1,256]{1,0:T(1,128)} %pixel_of.1), custom_call_target="tpu_custom_call" | custom-call | tf_op jit(solution)/shard_map/unmix/pallas_call | solution.py:435
  87.3 2.3 %copy.7 = f32[1,4,16,32,128]{4,3,2,1,0:T(8,128)} copy(f32[1,4,16,32,128]{4,3,2,1,0:T(8,128)} %bitcast.3) | data formatting | bytes 2097152

commit v6 on v5

--- a/solution.py
+++ b/solution.py
@@ -12,7 +12,7 @@
 MAP_W = 128
 MESH = pl.DeviceIdType.MESH
 LEVELS = 65534.0
-GROUPS = 8
+GROUPS = 4
 SPAN = 4096 // GROUPS
 
 time_step = 0.2
@@ -81,7 +81,10 @@
     x = chip % 4
     zh = f // 8
     y = p // 4
-    z = zh * 4 + p % 4
+    zl = p % 4
+    z = zh * 4 + zl
+    a = x + core * (y - x)
+    b = y + core * (x - y)
     sibling = (f + 1 - 2 * core, p)
 
     barrier = pltpu.get_barrier_semaphore()
@@ -118,7 +121,8 @@
     lanes = pl.ds(pl.multiple_of(p * 128, 128), 128)
 
     def tile_of(to):
-        return block.at[pl.ds(pl.multiple_of(to * 16, 16), 16), lanes]
+        tile = to // 8 * 8 + to % 4 * 2 + to // 4 % 2
+        return block.at[pl.ds(pl.multiple_of(tile * 16, 16), 16), lanes]
 
     load_own = pltpu.make_async_copy(tile_of(chip), cand.at[core, chip], load_sem.at[0])
     load_owner = pltpu.make_async_copy(owner_hbm, owner, load_sem.at[1])
@@ -154,16 +158,14 @@
     all_a.wait_recv()
     both = remote(cand.at[core], cand.at[core], b_send, b_recv, sibling)
     both.start()
-    all_a.wait_send()
     both.wait()
 
-    mine = pl.ds(pl.multiple_of(x * 16, 16), 16)
     for tt in range(2):
         o = owner[core + 2 * tt]
-        g[core, tt, p, zh, mine, :] = cand[o % 2, o // 2]
+        g[core, tt, zh // 2, a, b, zl, zh % 2] = cand[o % 2, o // 2]
 
     def along_z(i, _):
-        part = g.at[core, :, p, zh, mine, :]
+        part = g.at[core, :, zh // 2, a, b, zl, zh % 2]
         step = 8 + (i + 1) // 2 * (1 - i % 2 * 2)
         remote(part, part, z_send, z_recv, dev((z + step) % 16, x, core, y)).start()
         return _
@@ -172,10 +174,9 @@
     load_coefs.wait()
     for t in range(TURNS):
         coefs[t] = coefs_in[:, t, :].astype(jnp.float32).T
-    amount = g.at[0, 0, pl.ds(0, 15), 0, pl.ds(0, 32), :]
+    amount = templates.at[pl.ds(0, 240), pl.ds(0, 256)]
     all_z = remote(amount, amount, z_send, z_recv, sibling)
     all_z.wait_recv()
-    all_z.wait_send()
 
     def ring(stage, neighbour, region):
         def make(t, kind):
@@ -203,90 +204,30 @@
 
         return start, forward, finish, drain
 
-    def along(axis):
-        def neighbour(step):
-            if axis == "x":
-                return dev(z, (x + step) % 4, core, y)
-            return dev(z, x, core, (y + step) % 4)
-
-        return neighbour
-
-    def mid_region(axis):
-        def region(t, offset, half):
-            bx = (x + offset) % 4 if axis == "x" else x
-            by = (y + offset) % 4 if axis == "y" else y
-            points = pl.ds(by * 4, 4) if half is None else pl.ds(by * 4 + 2 * half, 2)
-            return (core, t // 2, points, pl.ds(t % 2 * 2, 2), pl.ds(pl.multiple_of(bx * 16, 16), 16), slice(None))
-
-        return region
-
-    def last_region(axis):
-        def region(t, offset, half):
-            if axis == "x":
-                points = pl.ds(0, 16) if half is None else pl.ds(8 * half, 8)
-                rows = pl.ds(pl.multiple_of((x + offset) % 4 * 16, 16), 16)
-            else:
-                by = (y + offset) % 4
-                points = pl.ds(by * 4, 4) if half is None else pl.ds(by * 4 + 2 * half, 2)
-                rows = slice(None)
-            return (core, t // 2, points, pl.ds(t % 2 * 2, 2), rows, slice(None))
-
-        return region
+    def first_neighbour(step):
+        return dev(z, (x + core * step) % 4, core, (y + (1 - core) * step) % 4)
+
+    def last_neighbour(step):
+        return dev(z, (x + (1 - core) * step) % 4, core, (y + core * step) % 4)
+
+    def mid_region(t, offset, half):
+        low = pl.ds(0, 4) if half is None else pl.ds(2 * half, 2)
+        return (core, t // 2, t % 2, a, (b + offset) % 4, low)
+
+    def last_region(t, offset, half):
+        firsts = pl.ds(0, 4) if half is None else pl.ds(2 * half, 2)
+        return (core, t // 2, t % 2, (a + offset) % 4, firsts)
 
     def swap(t):
-        part = g.at[core, t // 2, :, pl.ds(t % 2 * 2, 2)]
+        part = g.at[core, t // 2, t % 2]
         return remote(part, part, c_send.at[t], c_recv.at[t], sibling)
 
-    def rings(first, last):
-        return ring(0, along(first), mid_region(first)), ring(1, along(last), last_region(last))
-
-    def by_core(act):
-        @pl.when(core == 0)
-        def _even():
-            act(*rings("y", "x"))
-
-        @pl.when(core == 1)
-        def _odd():
-            act(*rings("x", "y"))
-
-    def open_mid(mid, last):
-        for t in range(TURNS):
-            mid[0](t)
-
-    def pass_mid(mid, last):
-        for t in range(TURNS):
-            mid[1](t)
-
-    def open_last(mid, last):
-        for t in range(TURNS):
-            mid[2](t)
-            if t < 2:
-                last[0](t)
-
-    def share(last, t):
+    mid = ring(0, first_neighbour, mid_region)
+    last = ring(1, last_neighbour, last_region)
+
+    def share(t):
         last[2](t)
         swap(t).start()
-
-    def first_half(mid, last):
-        last[1](0)
-        last[0](2)
-        last[1](1)
-        last[0](3)
-        share(last, 0)
-        last[1](2)
-        share(last, 1)
-
-    def middle(mid, last):
-        last[1](3)
-        share(last, 2)
-
-    def second_half(mid, last):
-        share(last, 3)
-
-    def close(mid, last):
-        for t in range(TURNS):
-            mid[3](t)
-            last[3](t)
 
     def send_rows(t, to):
         rows = pl.ds(pl.multiple_of(to * 16, 16), 16)
@@ -295,7 +236,10 @@
 
     def turn(t):
         for q in range(16):
-            templates[:, 128 * q : 128 * (q + 1)] = g[t % 2, t // 2, q].reshape(256, 128)
+            for k in range(8):
+                ends = (k % 4, q // 4) if t % 2 == 0 else (q // 4, k % 4)
+                tiles = g[t % 2, t // 2, k // 4, ends[0], ends[1], q % 4]
+                templates[32 * k : 32 * (k + 1), 128 * q : 128 * (q + 1)] = tiles.reshape(32, 128)
         gram = nt(templates[...], templates[...])
         step = 1.0 / jnp.sum(jnp.abs(gram), axis=1, keepdims=True)
         before = coefs[t]
@@ -348,22 +292,23 @@
             rest = (v - high.astype(jnp.float32)).astype(jnp.bfloat16)
             for h in range(GROUPS):
                 here = member[16 * h : 16 * h + 16, points]
-                parts[32 * h : 32 * h + 16, points] = high * here
-                parts[32 * h + 16 : 32 * h + 32, points] = rest * here
+                row = 64 * h + t % 2 * 16
+                parts[row : row + 16, points] = high * here
+                parts[row + 32 : row + 48, points] = rest * here
             return _
 
-        lax.fori_loop(0, 16, one, 0)
-
-    def place(t):
+        lax.fori_loop(0, 16, one, 0, unroll=4)
+
+    def place(pair):
         for n in range(SPAN // 256):
             placed = jnp.dot(
                 parts[...], select[:, 256 * n : 256 * (n + 1)], preferred_element_type=jnp.float32
             )
             for h in range(GROUPS):
-                whole = placed[32 * h : 32 * h + 16] + placed[32 * h + 16 : 32 * h + 32]
+                whole = placed[64 * h : 64 * h + 32] + placed[64 * h + 32 : 64 * h + 64]
                 for r in range(2):
                     row = h * (SPAN // 128) + 2 * n + r
-                    state[row, 16 * t : 16 * t + 16] = whole[:, 128 * r : 128 * (r + 1)]
+                    state[row, 32 * pair : 32 * pair + 32] = whole[:, 128 * r : 128 * (r + 1)]
 
     def flow(d):
         scaled = d * (1.0 / edge_scale)
@@ -385,23 +330,35 @@
             maps[rows, i, :] = u[i]
         return _
 
-    by_core(open_mid)
+    for t in range(TURNS):
+        mid[0](t)
     ids = remote(pixels.at[pl.ds(0, 15)], pixels.at[pl.ds(0, 15)], id_send, id_recv, sibling)
     load_pixels.wait()
     ids.wait_recv()
     lax.fori_loop(0, 4, spread, 0)
-    by_core(pass_mid)
+    for t in range(TURNS):
+        mid[1](t)
     lax.fori_loop(4, 8, spread, 0)
-    by_core(open_last)
+    for t in range(TURNS):
+        mid[2](t)
+        if t < 2:
+            last[0](t)
     lax.fori_loop(8, 16, spread, 0)
     load_residual.wait()
-    by_core(first_half)
+    last[1](0)
+    last[0](2)
+    last[1](1)
+    last[0](3)
+    share(0)
+    last[1](2)
+    share(1)
     swap(0).wait_recv()
     swap(1).wait_recv()
     turn(0)
-    by_core(middle)
+    last[1](3)
+    share(2)
     turn(1)
-    by_core(second_half)
+    share(3)
     swap(2).wait_recv()
     swap(3).wait_recv()
     turn(2)
@@ -415,15 +372,19 @@
             remote(rows, rows, s_send.at[t], s_recv.at[t], sibling),
         )
 
-    for t in range(TURNS):
-        for copies in sent(t):
-            copies.wait_recv()
-        split(t)
-        place(t)
-        lax.fori_loop(2 * t, 2 * t + 2, smooth, 0)
-    by_core(close)
+    for pair in range(2):
+        for t in (2 * pair, 2 * pair + 1):
+            for copies in sent(t):
+                copies.wait_recv()
+            split(t)
+        place(pair)
+        lax.fori_loop(4 * pair, 4 * pair + 4, smooth, 0)
+    all_a.wait_send()
+    all_z.wait_send()
     ids.wait_send()
     for t in range(TURNS):
+        mid[3](t)
+        last[3](t)
         swap(t).wait_send()
         for copies in sent(t):
             copies.wait_send()
@@ -446,14 +407,14 @@
             pltpu.VMEM((16, 1, 256), jnp.int32),
             pltpu.VMEM((256, TURNS, 256), jnp.bfloat16),
             pltpu.VMEM((TURNS, 256, 256), jnp.float32),
-            pltpu.VMEM((2, 2, 16, 4, 64, 128), jnp.bfloat16),
+            pltpu.VMEM((2, 2, 2, 4, 4, 4, 2, 16, 128), jnp.bfloat16),
             pltpu.VMEM((2, 16, 16, 128), jnp.bfloat16),
             pltpu.VMEM((256, 2048), jnp.bfloat16),
             pltpu.VMEM((256, 2048), jnp.bfloat16),
             pltpu.VMEM((TURNS, 256, 256), jnp.int16),
             pltpu.VMEM((16 * GROUPS, 4096), jnp.bfloat16),
             pltpu.VMEM((4096, SPAN), jnp.bfloat16),
-            pltpu.VMEM((32 * GROUPS, 4096), jnp.bfloat16),
+            pltpu.VMEM((64 * GROUPS, 4096), jnp.bfloat16),
             pltpu.VMEM((32, 64, 128), jnp.float32),
             dma,
             dma,

time: 90.2 us -> 84.3 us (0.935)
  Pallas kernels: 87.3 us -> 81.4 us
    pallas_call x1, Pallas kernels: 87.3 us -> 81.4 us  [unmix(): pl.pallas_call(unmix_kernel, name='unmix', out_shape=jax.ShapeDtypeStruct...]
where the time goes in v6:
time: 84.3 us; the launch traced here: 83.7 us
  Pallas kernels  81.4 us (97%)
  local copies, waits for them, and re-layouts  2.26 us (3%)
    pallas_call x1, Pallas kernels, unmix(): pl.pallas_call(unmix_kernel, name='unmix', out_shape=jax.ShapeDtypeStruct...  81.4 us
    unnamed x1, local copies, waits for them, and re-layouts  2.26 us

profile of v6, /device:TPU:1, one launch (start us, length us, event | category | flops | bytes accessed | tf_op | source)
XLA Modules:
  0.0 83.7 jit_solution(7431795040302567845)
XLA Ops:
  0.0 81.4 %unmix.1 = f32[64,32,128]{2,1,0:T(8,128)} custom-call(s32[32]{0:T(128)} %owner_hbm.1, bf16[256,2048]{1,0:T(8,128)(2,1)} %block.1, bf16[256,2048]{1,0:T(8,128)(2,1)} %bitcast.4, bf16[256,4,256]{2,1,0:T(4,128)(2,1)} %bitcast.5, s32[1,256]{1,0:T(1,128)} %pixel_of.1), custom_call_target="tpu_custom_call" | custom-call | tf_op jit(solution)/shard_map/unmix/pallas_call | solution.py:396
  81.4 2.3 %copy.7 = f32[1,4,16,32,128]{4,3,2,1,0:T(8,128)} copy(f32[1,4,16,32,128]{4,3,2,1,0:T(8,128)} %bitcast.3) | data formatting | bytes 2097152

commit v7 on v6

--- a/solution.py
+++ b/solution.py
@@ -33,13 +33,35 @@
     return lax.dot_general(a, b, (((1,), (1,)), ((), ())), preferred_element_type=jnp.float32)
 
 
+def flow(d):
+    scaled = d * (1.0 / edge_scale)
+    return d / (1.0 + scaled * scaled)
+
+
+def smooth(state, maps, group):
+    edge = lax.broadcasted_iota(jnp.int32, (32, 8, 128), 2) == 127
+    rows = pl.ds(pl.multiple_of(group * 8, 8), 8)
+    u = state[:, rows, :]
+    for repeat in range(SWEEPS):
+        right = jnp.where(edge, 0.0, flow(pltpu.roll(u, 127, 2) - u))
+        down = flow(u[1:] - u[:-1])
+        none = jnp.zeros((1, 8, 128), jnp.float32)
+        total = (right - pltpu.roll(right, 1, 2)) + (
+            jnp.concatenate([down, none], axis=0) - jnp.concatenate([none, down], axis=0)
+        )
+        u = u + time_step * total
+    for i in range(32):
+        maps[rows, i, :] = u[i]
+
+
 def unmix_kernel(
     owner_hbm,
     block,
     residual_hbm,
     coefs_hbm,
     pixel_of,
-    maps,
+    maps_hbm,
+    late_hbm,
     owner,
     codes,
     peaks,
@@ -55,7 +77,9 @@
     member,
     select,
     parts,
-    state,
+    early,
+    late,
+    maps,
     a_send,
     a_recv,
     b_send,
@@ -247,13 +271,15 @@
         peak = jnp.max(after, axis=1, keepdims=True)
         share_of_peak = after / jnp.where(peak > 0.0, peak, 1.0)
         updated[t] = (jnp.floor(share_of_peak * LEVELS + 0.5) - LEVELS / 2).astype(jnp.int32).astype(jnp.int16)
-        peaks[t, p] = jnp.broadcast_to(peak, (256, 128)).T[0:1]
+        peaks[t // 2, p, :, 256 * (t % 2) : 256 * (t % 2) + 256] = jnp.broadcast_to(peak, (256, 128)).T[0:1]
 
         def deliver(i, _):
             to = (p + i) % 16
             src, dst = send_rows(t, to)
             remote(src, dst, v_send.at[t], v_recv.at[t], (f, to)).start()
-            remote(peaks.at[t, p], peaks.at[t, p], s_send.at[t], s_recv.at[t], (f, to)).start()
+            if t % 2 == 1:
+                pair = peaks.at[t // 2, p]
+                remote(pair, pair, s_send.at[t // 2], s_recv.at[t // 2], (f, to)).start()
             return _
 
         lax.fori_loop(1, 16, deliver, 0)
@@ -280,7 +306,7 @@
         return _
 
     def split(t):
-        peak_cols[:, 0:16] = peaks[t].reshape(16, 256).T
+        peak_cols[:, 0:16] = peaks[t // 2, :, :, 256 * (t % 2) : 256 * (t % 2) + 256].reshape(16, 256).T
         own_peaks = peak_cols[pl.ds(pl.multiple_of(p * 16, 16), 16), :] * (1.0 / LEVELS)
         source = lax.broadcasted_iota(jnp.int32, (16, 128), 1)
 
@@ -308,27 +334,7 @@
                 whole = placed[64 * h : 64 * h + 32] + placed[64 * h + 32 : 64 * h + 64]
                 for r in range(2):
                     row = h * (SPAN // 128) + 2 * n + r
-                    state[row, 32 * pair : 32 * pair + 32] = whole[:, 128 * r : 128 * (r + 1)]
-
-    def flow(d):
-        scaled = d * (1.0 / edge_scale)
-        return d / (1.0 + scaled * scaled)
-
-    def smooth(group, _):
-        last = lax.broadcasted_iota(jnp.int32, (32, 8, 128), 2) == 127
-        rows = pl.ds(pl.multiple_of(group * 8, 8), 8)
-        u = state[:, rows, :]
-        for repeat in range(SWEEPS):
-            right = jnp.where(last, 0.0, flow(pltpu.roll(u, 127, 2) - u))
-            down = flow(u[1:] - u[:-1])
-            none = jnp.zeros((1, 8, 128), jnp.float32)
-            total = (right - pltpu.roll(right, 1, 2)) + (
-                jnp.concatenate([down, none], axis=0) - jnp.concatenate([none, down], axis=0)
-            )
-            u = u + time_step * total
-        for i in range(32):
-            maps[rows, i, :] = u[i]
-        return _
+                    (early, late)[pair][row] = whole[:, 128 * r : 128 * (r + 1)]
 
     for t in range(TURNS):
         mid[0](t)
@@ -366,19 +372,30 @@
 
     def sent(t):
         amount = codes.at[t, :, pl.ds(0, 15 * 256)]
-        rows = peaks.at[t, pl.ds(0, 15)]
-        return (
-            remote(amount, amount, v_send.at[t], v_recv.at[t], sibling),
-            remote(rows, rows, s_send.at[t], s_recv.at[t], sibling),
-        )
-
+        return remote(amount, amount, v_send.at[t], v_recv.at[t], sibling)
+
+    def sent_peaks(pair):
+        rows = peaks.at[pair, pl.ds(0, 15)]
+        return remote(rows, rows, s_send.at[pair], s_recv.at[pair], sibling)
+
+    store_maps = pltpu.make_async_copy(maps, maps_hbm, load_sem.at[5])
+    store_late = pltpu.make_async_copy(late, late_hbm, load_sem.at[6])
     for pair in range(2):
+        sent_peaks(pair).wait_recv()
         for t in (2 * pair, 2 * pair + 1):
-            for copies in sent(t):
-                copies.wait_recv()
+            sent(t).wait_recv()
             split(t)
         place(pair)
-        lax.fori_loop(4 * pair, 4 * pair + 4, smooth, 0)
+        if pair == 0:
+
+            def smooth_early(group, _):
+                smooth(early, maps, group)
+                return _
+
+            lax.fori_loop(0, 4, smooth_early, 0)
+            store_maps.start()
+        else:
+            store_late.start()
     all_a.wait_send()
     all_z.wait_send()
     ids.wait_send()
@@ -386,8 +403,11 @@
         mid[3](t)
         last[3](t)
         swap(t).wait_send()
-        for copies in sent(t):
-            copies.wait_send()
+        sent(t).wait_send()
+    for pair in range(2):
+        sent_peaks(pair).wait_send()
+    store_maps.wait()
+    store_late.wait()
 
 
 def unmix(owner_order, dictionary, residual, coefs, pixel_of):
@@ -396,13 +416,13 @@
     return pl.pallas_call(
         unmix_kernel,
         name="unmix",
-        out_shape=jax.ShapeDtypeStruct((64, 32, 128), jnp.float32),
+        out_shape=(jax.ShapeDtypeStruct((32, 32, 128), jnp.float32),) * 2,
         in_specs=[hbm] * 5,
-        out_specs=pl.BlockSpec(memory_space=pltpu.VMEM),
+        out_specs=(hbm,) * 2,
         scratch_shapes=[
             pltpu.SMEM((32,), jnp.int32),
             pltpu.VMEM((TURNS, 16, 4096), jnp.int16),
-            pltpu.VMEM((TURNS, 16, 1, 256), jnp.float32),
+            pltpu.VMEM((2, 16, 1, 512), jnp.float32),
             pltpu.VMEM((256, 128), jnp.float32),
             pltpu.VMEM((16, 1, 256), jnp.int32),
             pltpu.VMEM((256, TURNS, 256), jnp.bfloat16),
@@ -415,7 +435,9 @@
             pltpu.VMEM((16 * GROUPS, 4096), jnp.bfloat16),
             pltpu.VMEM((4096, SPAN), jnp.bfloat16),
             pltpu.VMEM((64 * GROUPS, 4096), jnp.bfloat16),
-            pltpu.VMEM((32, 64, 128), jnp.float32),
+            pltpu.VMEM((32, 32, 128), jnp.float32),
+            pltpu.VMEM((32, 32, 128), jnp.float32),
+            pltpu.VMEM((32, 32, 128), jnp.float32),
             dma,
             dma,
             dma,
@@ -432,14 +454,48 @@
             dma((TURNS,)),
             dma((TURNS,)),
             dma((TURNS,)),
-            dma((5,)),
+            dma((7,)),
         ],
         compiler_params=pltpu.CompilerParams(collective_id=0, has_side_effects=True, vmem_limit_bytes=60 << 20),
     )(owner_order, dictionary, residual, coefs, pixel_of)
 
 
+def finish_kernel(maps, late_hbm, out, late, smoothed, in_sems, out_sems):
+    reads = []
+    for group in range(4):
+        rows = pl.ds(8 * group, 8)
+        reads.append(pltpu.make_async_copy(late_hbm.at[:, rows], late.at[:, rows], in_sems.at[group]))
+        reads[group].start()
+    first = pltpu.make_async_copy(maps, out.at[pl.ds(0, 32)], out_sems.at[4])
+    first.start()
+    writes = []
+    for group in range(4):
+        reads[group].wait()
+        smooth(late, smoothed, group)
+        rows = pl.ds(8 * group, 8)
+        writes.append(pltpu.make_async_copy(smoothed.at[rows], out.at[pl.ds(32 + 8 * group, 8)], out_sems.at[group]))
+        writes[group].start()
+    for write in writes:
+        write.wait()
+    first.wait()
+
+
+def finish(maps, late):
+    hbm = pl.BlockSpec(memory_space=pltpu.HBM)
+    dma = pltpu.SemaphoreType.DMA
+    return pl.pallas_call(
+        finish_kernel,
+        name="finish",
+        out_shape=jax.ShapeDtypeStruct((64, 32, 128), jnp.float32),
+        in_specs=[hbm, hbm],
+        out_specs=hbm,
+        scratch_shapes=[pltpu.VMEM((32, 32, 128), jnp.float32)] * 2 + [dma((4,)), dma((5,))],
+        compiler_params=pltpu.CompilerParams(vmem_limit_bytes=60 << 20),
+    )(maps, late)
+
+
 def per_device(residual_in, coefs_in, dictionary, owner_order, pixel_of):
-    maps = unmix(owner_order, dictionary, residual_in[0], coefs_in[0], pixel_of)
+    maps = finish(*unmix(owner_order, dictionary, residual_in[0], coefs_in[0], pixel_of))
     return maps.reshape(1, TURNS, 16, 32, MAP_W)
 
 

time: 84.3 us -> 96.6 us (1.15)
  Pallas kernels: 81.4 us -> 96.1 us
  local copies, waits for them, and re-layouts: 2.26 us -> 0 us
    pallas_call x1 -> x2, Pallas kernels: 81.4 us -> 96.1 us  [the longest x1 79 us: unmix(): pl.pallas_call(unmix_kernel, name='unmix', out_shape=(jax.ShapeDtypeStruc...]
    unnamed x1 -> x0, local copies, waits for them, and re-layouts: 2.26 us -> none
where the time goes in v7:
time: 96.6 us; the launch traced here: 96.3 us
  Pallas kernels  96.1 us (99%)
    pallas_call x1, Pallas kernels, unmix(): pl.pallas_call(unmix_kernel, name='unmix', out_shape=(jax.ShapeDtypeStruc...  79 us
    pallas_call x1, Pallas kernels, finish(): pl.pallas_call(finish_kernel, name='finish', out_shape=jax.ShapeDtypeStru...  17.1 us

profile of v7, /device:TPU:1, one launch (start us, length us, event | category | flops | bytes accessed | tf_op | source)
XLA Modules:
  0.0 96.3 jit_solution(3878406449776792782)
XLA Ops:
  0.0 79.0 %unmix.1 = (f32[32,32,128]{2,1,0:T(8,128)}, f32[32,32,128]{2,1,0:T(8,128)}) custom-call(s32[32]{0:T(128)} %owner_hbm.1, bf16[256,2048]{1,0:T(8,128)(2,1)} %block.1, bf16[256,2048]{1,0:T(8,128)(2,1)} %bitcast.3, bf16[256,4,256]{2,1,0:T(4,128)(2,1)} %bitcast.4, s32[1,256]{1,0:T(1,128)} %pixel_of.1), custom_call_target="tpu_custom_call" | custom-call | tf_op jit(solution)/shard_map/unmix/pallas_call | solution.py:416
  79.0 17.1 %finish.1 = f32[64,32,128]{2,1,0:T(8,128)} custom-call(f32[32,32,128]{2,1,0:T(8,128)} %get-tuple-element.7.maps, f32[32,32,128]{2,1,0:T(8,128)} %get-tuple-element.8.late_hbm), custom_call_target="tpu_custom_call" | custom-call | tf_op jit(solution)/shard_map/finish/pallas_call | solution.py:486

commit v8 on v7

--- a/solution.py
+++ b/solution.py
@@ -41,7 +41,7 @@
 def smooth(state, maps, group):
     edge = lax.broadcasted_iota(jnp.int32, (32, 8, 128), 2) == 127
     rows = pl.ds(pl.multiple_of(group * 8, 8), 8)
-    u = state[:, rows, :]
+    u = state[group]
     for repeat in range(SWEEPS):
         right = jnp.where(edge, 0.0, flow(pltpu.roll(u, 127, 2) - u))
         down = flow(u[1:] - u[:-1])
@@ -188,19 +188,24 @@
         o = owner[core + 2 * tt]
         g[core, tt, zh // 2, a, b, zl, zh % 2] = cand[o % 2, o // 2]
 
-    def along_z(i, _):
-        part = g.at[core, :, zh // 2, a, b, zl, zh % 2]
-        step = 8 + (i + 1) // 2 * (1 - i % 2 * 2)
-        remote(part, part, z_send, z_recv, dev((z + step) % 16, x, core, y)).start()
-        return _
-
-    lax.fori_loop(0, 15, along_z, 0)
+    def along_z(tt):
+        def one(i, _):
+            part = g.at[core, tt, zh // 2, a, b, zl, zh % 2]
+            step = 8 + (i + 1) // 2 * (1 - i % 2 * 2)
+            remote(part, part, z_send.at[tt], z_recv.at[tt], dev((z + step) % 16, x, core, y)).start()
+            return _
+
+        lax.fori_loop(0, 15, one, 0)
+
+    def all_z(tt):
+        amount = templates.at[pl.ds(0, 240), pl.ds(0, 128)]
+        return remote(amount, amount, z_send.at[tt], z_recv.at[tt], sibling)
+
+    along_z(0)
+    along_z(1)
     load_coefs.wait()
     for t in range(TURNS):
         coefs[t] = coefs_in[:, t, :].astype(jnp.float32).T
-    amount = templates.at[pl.ds(0, 240), pl.ds(0, 256)]
-    all_z = remote(amount, amount, z_send, z_recv, sibling)
-    all_z.wait_recv()
 
     def ring(stage, neighbour, region):
         def make(t, kind):
@@ -334,22 +339,32 @@
                 whole = placed[64 * h : 64 * h + 32] + placed[64 * h + 32 : 64 * h + 64]
                 for r in range(2):
                     row = h * (SPAN // 128) + 2 * n + r
-                    (early, late)[pair][row] = whole[:, 128 * r : 128 * (r + 1)]
-
-    for t in range(TURNS):
-        mid[0](t)
+                    for group in range(4):
+                        (early, late)[pair][group, row] = whole[8 * group : 8 * group + 8, 128 * r : 128 * (r + 1)]
+
+    all_z(0).wait_recv()
+    mid[0](0)
+    mid[0](1)
+    all_z(1).wait_recv()
+    mid[0](2)
+    mid[0](3)
     ids = remote(pixels.at[pl.ds(0, 15)], pixels.at[pl.ds(0, 15)], id_send, id_recv, sibling)
     load_pixels.wait()
     ids.wait_recv()
-    lax.fori_loop(0, 4, spread, 0)
-    for t in range(TURNS):
-        mid[1](t)
-    lax.fori_loop(4, 8, spread, 0)
-    for t in range(TURNS):
-        mid[2](t)
-        if t < 2:
-            last[0](t)
-    lax.fori_loop(8, 16, spread, 0)
+    lax.fori_loop(0, 3, spread, 0)
+    mid[1](0)
+    mid[1](1)
+    lax.fori_loop(3, 5, spread, 0)
+    mid[1](2)
+    mid[1](3)
+    lax.fori_loop(5, 7, spread, 0)
+    mid[2](0)
+    last[0](0)
+    mid[2](1)
+    last[0](1)
+    lax.fori_loop(7, 16, spread, 0)
+    mid[2](2)
+    mid[2](3)
     load_residual.wait()
     last[1](0)
     last[0](2)
@@ -397,7 +412,8 @@
         else:
             store_late.start()
     all_a.wait_send()
-    all_z.wait_send()
+    all_z(0).wait_send()
+    all_z(1).wait_send()
     ids.wait_send()
     for t in range(TURNS):
         mid[3](t)
@@ -416,7 +432,10 @@
     return pl.pallas_call(
         unmix_kernel,
         name="unmix",
-        out_shape=(jax.ShapeDtypeStruct((32, 32, 128), jnp.float32),) * 2,
+        out_shape=(
+            jax.ShapeDtypeStruct((32, 32, 128), jnp.float32),
+            jax.ShapeDtypeStruct((4, 32, 8, 128), jnp.float32),
+        ),
         in_specs=[hbm] * 5,
         out_specs=(hbm,) * 2,
         scratch_shapes=[
@@ -435,15 +454,15 @@
             pltpu.VMEM((16 * GROUPS, 4096), jnp.bfloat16),
             pltpu.VMEM((4096, SPAN), jnp.bfloat16),
             pltpu.VMEM((64 * GROUPS, 4096), jnp.bfloat16),
-            pltpu.VMEM((32, 32, 128), jnp.float32),
-            pltpu.VMEM((32, 32, 128), jnp.float32),
+            pltpu.VMEM((4, 32, 8, 128), jnp.float32),
+            pltpu.VMEM((4, 32, 8, 128), jnp.float32),
             pltpu.VMEM((32, 32, 128), jnp.float32),
             dma,
             dma,
             dma,
             dma,
-            dma,
-            dma,
+            dma((2,)),
+            dma((2,)),
             dma((2, 4, TURNS)),
             dma((2, 4, TURNS)),
             dma((TURNS,)),
@@ -460,14 +479,14 @@
     )(owner_order, dictionary, residual, coefs, pixel_of)
 
 
-def finish_kernel(maps, late_hbm, out, late, smoothed, in_sems, out_sems):
+def finish_kernel(maps_hbm, late_hbm, out, maps, late, smoothed, in_sems, out_sems):
     reads = []
     for group in range(4):
-        rows = pl.ds(8 * group, 8)
-        reads.append(pltpu.make_async_copy(late_hbm.at[:, rows], late.at[:, rows], in_sems.at[group]))
+        reads.append(pltpu.make_async_copy(late_hbm.at[group], late.at[group], in_sems.at[group]))
         reads[group].start()
+    read_maps = pltpu.make_async_copy(maps_hbm, maps, in_sems.at[4])
+    read_maps.start()
     first = pltpu.make_async_copy(maps, out.at[pl.ds(0, 32)], out_sems.at[4])
-    first.start()
     writes = []
     for group in range(4):
         reads[group].wait()
@@ -475,6 +494,9 @@
         rows = pl.ds(8 * group, 8)
         writes.append(pltpu.make_async_copy(smoothed.at[rows], out.at[pl.ds(32 + 8 * group, 8)], out_sems.at[group]))
         writes[group].start()
+        if group == 0:
+            read_maps.wait()
+            first.start()
     for write in writes:
         write.wait()
     first.wait()
@@ -489,7 +511,13 @@
         out_shape=jax.ShapeDtypeStruct((64, 32, 128), jnp.float32),
         in_specs=[hbm, hbm],
         out_specs=hbm,
-        scratch_shapes=[pltpu.VMEM((32, 32, 128), jnp.float32)] * 2 + [dma((4,)), dma((5,))],
+        scratch_shapes=[
+            pltpu.VMEM((32, 32, 128), jnp.float32),
+            pltpu.VMEM((4, 32, 8, 128), jnp.float32),
+            pltpu.VMEM((32, 32, 128), jnp.float32),
+            dma((5,)),
+            dma((5,)),
+        ],
         compiler_params=pltpu.CompilerParams(vmem_limit_bytes=60 << 20),
     )(maps, late)
 

time: 96.6 us -> 81.6 us (0.84)
  Pallas kernels: 96.1 us -> 81.3 us
    pallas_call x1, Pallas kernels: 17.1 us -> 4.43 us  [finish(): pl.pallas_call(finish_kernel, name='finish', out_shape=jax.ShapeDtypeStru...]
    pallas_call x1, Pallas kernels: 79 us -> 76.9 us  [unmix(): pl.pallas_call(unmix_kernel, name='unmix', out_shape=(jax.ShapeDtypeStruc...]
where the time goes in v8:
time: 81.6 us; the launch traced here: 81.5 us
  Pallas kernels  81.3 us (100%)
    pallas_call x1, Pallas kernels, unmix(): pl.pallas_call(unmix_kernel, name='unmix', out_shape=(jax.ShapeDtypeStruc...  76.9 us
    pallas_call x1, Pallas kernels, finish(): pl.pallas_call(finish_kernel, name='finish', out_shape=jax.ShapeDtypeStru...  4.43 us

profile of v8, /device:TPU:1, one launch (start us, length us, event | category | flops | bytes accessed | tf_op | source)
XLA Modules:
  0.0 81.5 jit_solution(17717104990986331744)
XLA Ops:
  0.0 76.9 %unmix.1 = (f32[32,32,128]{2,1,0:T(8,128)}, f32[4,32,8,128]{3,2,1,0:T(8,128)}) custom-call(s32[32]{0:T(128)} %owner_hbm.1, bf16[256,2048]{1,0:T(8,128)(2,1)} %block.1, bf16[256,2048]{1,0:T(8,128)(2,1)} %bitcast.3, bf16[256,4,256]{2,1,0:T(4,128)(2,1)} %bitcast.4, s32[1,256]{1,0:T(1,128)} %pixel_of.1), custom_call_target="tpu_custom_call" | custom-call | tf_op jit(solution)/shard_map/unmix/pallas_call | solution.py:432
  76.9 4.4 %finish.1 = f32[64,32,128]{2,1,0:T(8,128)} custom-call(f32[32,32,128]{2,1,0:T(8,128)} %get-tuple-element.7.maps_hbm, f32[4,32,8,128]{3,2,1,0:T(8,128)} %get-tuple-element.8.late_hbm), custom_call_target="tpu_custom_call" | custom-call | tf_op jit(solution)/shard_map/finish/pallas_call | solution.py:508
